TPU v7x, 128 devices: a whole 4x4x4 slice. The times are simulated.
128 devices in a mesh: dp: 8 (over z, y_lo), tensor: 16 (over x, y_hi, core).
Axes of the slice: x: 4, y: 4 (y_hi: 2, y_lo: 2; y = y_hi * 2 + y_lo), z: 4, core: 2. Of those that a mesh axis runs over, the one named last changes fastest.
Arguments:
- activations: bfloat16 [256, 8192], P('dp'), may hold values from -6 to 6
- query_weight: bfloat16 [8192, 8192], P(None, 'tensor'), may hold values from -0.0625 to 0.0625
- output_weight: bfloat16 [8192, 8192], P('tensor'), may hold values from -0.375 to 0.375
- key_cache: bfloat16 [256, 8, 1024, 128], P(('dp', 'tensor'))
- value_cache: bfloat16 [256, 8, 1024, 128], P(('dp', 'tensor')), may hold values from -6 to 6
- fresh_pair: bfloat16 [256, 2, 1024], P(('dp', 'tensor')), may hold values from -6 to 6
- cache_length: int32 [256], P(('dp', 'tensor')), may hold values from 2 to 1024
- row_tenant: int32 [256], P('dp'), may hold values from 0 to 63, as said below
- tenant_slot: int32 [64], replicated, may hold values from 0 to 63, as said below
- query_deltas: bfloat16 [64, 128, 128, 128], P('dp', 'tensor'), may hold values from -0.1796875 to 0.1796875
- query_where: int32 [64, 128], P('dp', 'tensor'), may hold values from 0 to 255, as said below
- output_deltas: bfloat16 [64, 128, 128, 128], P('dp', 'tensor'), may hold values from -0.71875 to 0.71875
- output_where: int32 [64, 128], P('dp', 'tensor'), may hold values from 0 to 255, as said below
Outputs:
- layer_out: bfloat16 [256, 8192], P('dp', 'tensor')
Inputs may be any that keep to these rules, and one draw needn't show every extreme that they name: A permutation: tenant t's tiles sit in slot tenant_slot[t], on dp index tenant_slot[t] // 8. `row_tenant`: among the requests of one dp group (32 consecutive rows), at most 8 have tenants stored on one dp index; one store receives exactly 8 from every group. `query_where`: within each block of 8 entries (one slot, one shard) the places are distinct. `output_where`: within each block of 8 entries (one slot, one shard) the places are distinct.
All inputs are finite; a program needn't handle non-finite values.
Results may differ from a plain program's by a relative error of at most 0.0089.
Values may be sent and summed in bfloat16 or wider, within the bound.
No kernel may reach another device: no remote copies, remote signals or barrier semaphores. Data moves between devices by JAX's collectives and lax.ppermute only.
A program may use at most 192 MiB of HBM per device.

v0:
```python
import jax
import jax.numpy as jnp
from jax import lax
from jax.sharding import PartitionSpec as P


def apply_tiles(inputs, row_slot, deltas, where_list, first_slot, out_columns):
    tile_size = deltas.shape[-1]
    slot_count = where_list.shape[0]
    per_slot = where_list.shape[1]
    out_tiles = out_columns // tile_size
    count_rows = inputs.shape[0]
    in_tiles = inputs.shape[1] // tile_size
    blocks = inputs.reshape(count_rows, in_tiles, tile_size)
    flat_places = where_list.reshape(slot_count * per_slot)
    source = flat_places // out_tiles
    target = flat_places % out_tiles
    pick_table = (source[:, None] == jnp.arange(in_tiles, dtype=jnp.int32)[None, :]).astype(
        inputs.dtype
    )
    picked = jnp.einsum(
        "rbt,kb->rkt", blocks, pick_table, preferred_element_type=jnp.float32
    ).astype(inputs.dtype)
    owners = first_slot + jnp.arange(slot_count * per_slot, dtype=jnp.int32) // per_slot
    chosen = row_slot[:, None] == owners[None, :]
    picked = jnp.where(chosen[:, :, None], picked, jnp.zeros((), inputs.dtype))
    flat_tiles = deltas.reshape(slot_count * per_slot, tile_size, tile_size)
    products = jnp.einsum("rkt,kts->rks", picked, flat_tiles, preferred_element_type=jnp.float32)
    spread = (target[:, None] == jnp.arange(out_tiles, dtype=jnp.int32)[None, :]).astype(
        jnp.float32
    )
    combined = jnp.einsum("rks,kb->rbs", products, spread, precision=lax.Precision.HIGHEST)
    return combined.reshape(count_rows, out_columns)


def dispatch_table(row_slot, per_store, stores, capacity):
    store_of = row_slot // per_store
    row_order = jnp.arange(row_slot.shape[0], dtype=jnp.int32)
    earlier = (store_of[:, None] == store_of[None, :]) & (row_order[None, :] < row_order[:, None])
    place_in = jnp.sum(earlier.astype(jnp.int32), axis=1)
    place_at = store_of * capacity + place_in
    one_hot = place_at[None, :] == jnp.arange(stores * capacity, dtype=jnp.int32)[:, None]
    return (place_at, one_hot)


def visit_store(inputs, row_slot, one_hot, deltas, where_list, out_columns, capacity):
    stores = lax.axis_size("dp")
    packed = jnp.dot(
        one_hot.astype(inputs.dtype), inputs, preferred_element_type=jnp.float32
    ).astype(inputs.dtype)
    slot_sent = jnp.max(jnp.where(one_hot, row_slot[None, :], -1), axis=1)
    packed = packed.reshape(stores, capacity, inputs.shape[1])
    slot_sent = slot_sent.reshape(stores, capacity)
    arrived, arrived_slot = (
        lax.all_to_all(packed, "dp", split_axis=0, concat_axis=0, tiled=True),
        lax.all_to_all(slot_sent, "dp", split_axis=0, concat_axis=0, tiled=True),
    )
    first_slot = lax.axis_index("dp") * deltas.shape[0]
    result = apply_tiles(
        arrived.reshape(stores * capacity, inputs.shape[1]),
        arrived_slot.reshape(stores * capacity),
        deltas,
        where_list,
        first_slot,
        out_columns,
    )
    return result.reshape(stores, capacity, out_columns)


def return_home(result, one_hot):
    returned = lax.all_to_all(result, "dp", split_axis=0, concat_axis=0, tiled=True)
    flattened = returned.reshape(returned.shape[0] * returned.shape[1], returned.shape[2])
    return jnp.dot(one_hot.astype(jnp.float32).T, flattened, precision=lax.Precision.HIGHEST)


def attend(query_rows, key_cache, value_cache, fresh_pair, cache_length):
    count_rows, kv_heads, context, head_dim = key_cache.shape
    grouped = query_rows.reshape(count_rows, kv_heads, -1, head_dim)
    score_scale = head_dim ** (-0.5)
    scores = (
        jnp.einsum("rkgd,rkld->rkgl", grouped, key_cache, preferred_element_type=jnp.float32)
        * score_scale
    )
    fresh_key = fresh_pair[:, 0].reshape(count_rows, kv_heads, head_dim)
    fresh_value = fresh_pair[:, 1].reshape(count_rows, kv_heads, head_dim).astype(jnp.float32)
    own_score = (
        jnp.einsum("rkgd,rkd->rkg", grouped, fresh_key, preferred_element_type=jnp.float32)
        * score_scale
    )
    position = jnp.arange(context, dtype=jnp.int32)
    visible = (position[None, :] < cache_length[:, None])[:, None, None, :]
    scores = jnp.where(visible, scores, -1e30)
    highest = jnp.maximum(jnp.max(scores, axis=3), own_score)
    weights = jnp.where(visible, jnp.exp(scores - highest[..., None]), 0.0)
    own_weight = jnp.exp(own_score - highest)
    denominator = jnp.sum(weights, axis=3) + own_weight
    probabilities = (weights / denominator[..., None]).astype(jnp.bfloat16)
    own_probability = (own_weight / denominator).astype(jnp.bfloat16)
    mixed = jnp.einsum(
        "rkgl,rkld->rkgd", probabilities, value_cache, preferred_element_type=jnp.float32
    )
    mixed = mixed + own_probability.astype(jnp.float32)[..., None] * fresh_value[:, :, None, :]
    return mixed.astype(jnp.bfloat16).reshape(count_rows, -1)


def body(
    activations,
    query_weight,
    output_weight,
    key_cache,
    value_cache,
    fresh_pair,
    cache_length,
    row_tenant,
    tenant_slot,
    query_deltas,
    query_where,
    output_deltas,
    output_where,
):
    group_rows = activations.shape[0]
    stores = lax.axis_size("dp")
    capacity = max(2, 2 * group_rows // stores)
    per_store = query_deltas.shape[0]
    row_slot = jnp.take(tenant_slot, row_tenant)
    place_at, one_hot = dispatch_table(row_slot, per_store, stores, capacity)
    query_width = query_weight.shape[1]
    out_columns = output_weight.shape[1]
    base_query = jnp.dot(activations, query_weight, preferred_element_type=jnp.float32)
    query_extra = return_home(
        visit_store(
            activations, row_slot, one_hot, query_deltas, query_where, query_width, capacity
        ),
        one_hot,
    )
    query_heads = (base_query + query_extra).astype(jnp.bfloat16)
    query_rows = lax.all_to_all(query_heads, "tensor", split_axis=0, concat_axis=1, tiled=True)
    attended = attend(query_rows, key_cache, value_cache, fresh_pair, cache_length)
    heads_out = lax.all_to_all(attended, "tensor", split_axis=1, concat_axis=0, tiled=True)
    base_out = jnp.dot(heads_out, output_weight, preferred_element_type=jnp.float32)
    visited = visit_store(
        heads_out, row_slot, one_hot, output_deltas, output_where, out_columns, capacity
    )
    partial_terms = base_out + return_home(visited, one_hot)
    summed = lax.psum_scatter(partial_terms, "tensor", scatter_dimension=1, tiled=True)
    return summed.astype(jnp.bfloat16)


def solution(mesh):
    placed = (
        P("dp", None),
        P(None, "tensor"),
        P("tensor", None),
        P(("dp", "tensor"), None, None, None),
        P(("dp", "tensor"), None, None, None),
        P(("dp", "tensor"), None, None),
        P(("dp", "tensor")),
        P("dp"),
        P(),
        P("dp", "tensor", None, None),
        P("dp", "tensor"),
        P("dp", "tensor", None, None),
        P("dp", "tensor"),
    )
    return jax.shard_map(
        body, mesh=mesh, in_specs=placed, out_specs=P("dp", "tensor"), check_vma=False
    )
```

profile of v0, /device:TPU:1, one launch (start us, length us, event | category | flops | bytes accessed | tf_op | source)
XLA Modules:
  0.0 214.8 jit_solution(2485666070460402730)
XLA Ops:
  6.5 0.0 copy-start
  6.5 0.0 copy-start.4
  6.5 0.8 compare_select_fusion
  7.4 0.0 copy-start.1
  7.4 1.4 gather_fusion
  8.8 0.7 and_select_fusion.5
  9.5 0.2 convert_reduce_fusion
  9.6 0.1 select_reduce_fusion
  9.7 0.7 all_to_all.45
  10.4 6.9 %all-to-all-start = ((s32[8,1,8]{2,1,0:T(1,128)}), s32[8,1,8]{2,1,0:T(1,128)S(1)}, u32[]{:S(2)}, u32[]{:S(2)}) async-start(s32[8,1,8]{2,1,0:T(1,128)} %bitcast.1), calls=%async_computation | async-start | bytes 8192 | tf_op jit(solution)/shard_map/all_to_all | solution.py:56
  17.3 2.6 %fusion = bf16[8,8,8192]{2,1,0:T(8,128)(2,1)} fusion(bf16[32,8192]{1,0:T(8,128)(2,1)} %param.13, s32[32]{0:T(128)S(1)} %multiply_add_fusion), kind=kOutput, calls=%fused_computation.2 | convolution fusion | flops 34080768 | bytes 1572992 | tf_op jit(solution)/shard_map/dot_general | solution.py:48
  19.9 0.0 copy-done.4
  19.9 0.1 reshape.265
  20.0 2.3 %all-to-all-done = s32[8,1,8]{2,1,0:T(1,128)S(1)} async-done(((s32[8,1,8]{2,1,0:T(1,128)}), s32[8,1,8]{2,1,0:T(1,128)S(1)}, u32[]{:S(2)}, u32[]{:S(2)}) %all-to-all-start) | async-done | bytes 288 | tf_op jit(solution)/shard_map/all_to_all | solution.py:56
  22.2 4.2 %all-to-all-start.1 = ((bf16[8,8,8192]{2,1,0:T(8,128)(2,1)}), bf16[8,8,8192]{2,1,0:T(8,128)(2,1)}, u32[]{:S(2)}, u32[]{:S(2)}) async-start(bf16[8,8,8192]{2,1,0:T(8,128)(2,1)} %fusion), calls=%async_computation.1 | async-start | bytes 2097152 | tf_op jit(solution)/shard_map/all_to_all | solution.py:55
  26.5 0.0 copy-done.1
  26.5 4.9 %fusion.53 = f32[32,512]{1,0:T(8,128)S(1)} fusion(bf16[32,8192]{1,0:T(8,128)(2,1)S(1)} %copy-done.1, bf16[8192,512]{1,0:T(8,128)(2,1)} %param.14), kind=kOutput, calls=%fused_computation.94 | convolution fusion | flops 268435456 | bytes 8978432 | tf_op jit(solution)/shard_map/dot_general | solution.py:129
  31.4 0.5 broadcast.255
  32.0 0.7 reduce.3
  32.6 0.1 eq.116
  32.7 0.1 broadcast_compare_fusion
  32.8 7.5 %all-to-all-done.1 = bf16[8,8,8192]{2,1,0:T(8,128)(2,1)} async-done(((bf16[8,8,8192]{2,1,0:T(8,128)(2,1)}), bf16[8,8,8192]{2,1,0:T(8,128)(2,1)}, u32[]{:S(2)}, u32[]{:S(2)}) %all-to-all-start.1) | async-done | bytes 1048608 | tf_op jit(solution)/shard_map/all_to_all | solution.py:55
  40.3 1.5 copy.33
  41.8 0.8 fusion.10
  42.6 0.0 copy-done
  42.6 1.3 convolution_bitcast_fusion.1
  43.9 0.0 copy-start.3
  43.9 2.0 fusion.14
  45.9 0.7 reshape_reshape.13
  46.6 3.7 %all-to-all-start.2 = ((f32[8,8,512]{2,1,0:T(8,128)}), f32[8,8,512]{2,1,0:T(8,128)S(1)}, u32[]{:S(2)}, u32[]{:S(2)}) async-start(f32[8,8,512]{2,1,0:T(8,128)} %reshape_reshape.13), calls=%async_computation.2 | async-start | bytes 262144 | tf_op jit(solution)/shard_map/all_to_all | solution.py:71
  50.3 0.0 copy-done.3
  50.3 5.5 %all-to-all-done.2 = f32[8,8,512]{2,1,0:T(8,128)S(1)} async-done(((f32[8,8,512]{2,1,0:T(8,128)}), f32[8,8,512]{2,1,0:T(8,128)S(1)}, u32[]{:S(2)}, u32[]{:S(2)}) %all-to-all-start.2) | async-done | bytes 131104 | tf_op jit(solution)/shard_map/all_to_all | solution.py:71
  55.8 0.2 fusion.18
  56.1 0.6 all_to_all.49
  56.7 10.3 %all-to-all-start.3 = ((bf16[16,2,512]{2,1,0:T(2,128)(2,1)}), bf16[16,2,512]{2,1,0:T(2,128)(2,1)S(1)}, u32[]{:S(2)}, u32[]{:S(2)}) async-start(bf16[16,2,512]{2,1,0:T(2,128)(2,1)} %all_to_all.49), calls=%async_computation.3 | async-start | bytes 65536 | tf_op jit(solution)/shard_map/all_to_all | solution.py:137
  67.0 0.0 copy-done.6
  67.0 0.1 iota_compare_fusion.8
  67.1 7.2 %all-to-all-done.3 = bf16[16,2,512]{2,1,0:T(2,128)(2,1)S(1)} async-done(((bf16[16,2,512]{2,1,0:T(2,128)(2,1)}), bf16[16,2,512]{2,1,0:T(2,128)(2,1)S(1)}, u32[]{:S(2)}, u32[]{:S(2)}) %all-to-all-start.3) | async-done | bytes 32800 | tf_op jit(solution)/shard_map/all_to_all | solution.py:137
  74.4 0.1 fusion.35
  74.5 3.6 %fusion.52 = (f32[2,8,8]{2,1,0:T(8,128)S(1)}, f32[2,8,8,1024]{3,2,1,0:T(8,128)S(1)}) fusion(bf16[2,8,8,128]{3,2,1,0:T(8,128)(2,1)S(1)} %reshape.269, bf16[2,8,1024,128]{3,2,1,0:T(8,128)(2,1)} %param.16, pred[2,1024]{1,0:T(4,128)(4,1)S(1)} %iota_compare_fusion.8), kind=kOutput, calls=%fused_computation.93 | convolution fusion | flops 33947520 | bytes 4753920 | tf_op jit(solution)/shard_map/rkgd,rkld->rkgl/dot_general | solution.py:81
  78.1 0.2 fusion.22
  78.4 0.0 copy-done.2
  78.4 0.0 copy-start.5
  78.4 0.7 fusion.19
  79.2 0.6 copy.28
  79.8 3.7 %all-to-all-start.4 = ((bf16[2,16,512]{2,0,1:T(2,128)(2,1)}), bf16[2,16,512]{2,0,1:T(2,128)(2,1)S(1)}, u32[]{:S(2)}, u32[]{:S(2)}) async-start(bf16[2,16,512]{2,0,1:T(2,128)(2,1)} %copy.28), calls=%async_computation.4 | async-start | bytes 65536 | tf_op jit(solution)/shard_map/all_to_all | solution.py:139
  83.5 0.0 copy-done.5
  83.5 0.1 reshape.270
  83.6 7.3 %all-to-all-done.4 = bf16[2,16,512]{2,0,1:T(2,128)(2,1)S(1)} async-done(((bf16[2,16,512]{2,0,1:T(2,128)(2,1)}), bf16[2,16,512]{2,0,1:T(2,128)(2,1)S(1)}, u32[]{:S(2)}, u32[]{:S(2)}) %all-to-all-start.4) | async-done | bytes 32800 | tf_op jit(solution)/shard_map/all_to_all | solution.py:139
  90.9 0.9 fusion.17
  91.8 3.5 %all-to-all-start.5 = ((bf16[8,8,512]{2,1,0:T(8,128)(2,1)}), bf16[8,8,512]{2,1,0:T(8,128)(2,1)S(1)}, u32[]{:S(2)}, u32[]{:S(2)}) async-start(bf16[8,8,512]{2,1,0:T(8,128)(2,1)} %fusion.17), calls=%async_computation.5 | async-start | bytes 131072 | tf_op jit(solution)/shard_map/all_to_all | solution.py:55
  95.4 5.1 %all-to-all-done.5 = bf16[8,8,512]{2,1,0:T(8,128)(2,1)S(1)} async-done(((bf16[8,8,512]{2,1,0:T(8,128)(2,1)}), bf16[8,8,512]{2,1,0:T(8,128)(2,1)S(1)}, u32[]{:S(2)}, u32[]{:S(2)}) %all-to-all-start.5) | async-done | bytes 65568 | tf_op jit(solution)/shard_map/all_to_all | solution.py:55
  100.5 1.0 fusion.12
  101.5 2.9 %convolution_bitcast_fusion = f32[64,64,128]{2,0,1:T(8,128)S(1)} fusion(bf16[64,128,128]{2,1,0:T(8,128)(2,1)} %bitcast.70, bf16[64,64,128]{2,1,0:T(8,128)(2,1)S(1)} %fusion.12), kind=kOutput, calls=%fused_computation.10 | convolution fusion | flops 134217728 | bytes 5242880 | tf_op jit(solution)/shard_map/rkt,kts->rks/dot_general | solution.py:28
  104.4 3.8 %fusion.6 = f32[64,64,128]{2,1,0:T(8,128)} fusion(f32[64,64,128]{2,0,1:T(8,128)S(1)} %convolution_bitcast_fusion, s32[64]{0:T(128)S(1)} %get-tuple-element.9), kind=kOutput, calls=%fused_computation.9 | convolution fusion | flops 402657280 | bytes 4194560 | tf_op jit(solution)/shard_map/rks,kb->rbs/dot_general | solution.py:32
  108.2 2.7 %reshape_reshape.15 = f32[8,8,8192]{2,1,0:T(8,128)} reshape(f32[64,64,128]{2,1,0:T(8,128)} %fusion.6) | data formatting | bytes 4194304 | tf_op jit(solution)/shard_map/reshape;reshape | solution.py:67
  110.9 4.4 %all-to-all-start.6 = ((f32[8,8,8192]{2,1,0:T(8,128)}), f32[8,8,8192]{2,1,0:T(8,128)}, u32[]{:S(2)}, u32[]{:S(2)}) async-start(f32[8,8,8192]{2,1,0:T(8,128)} %reshape_reshape.15), calls=%async_computation.6 | async-start | bytes 4194304 | tf_op jit(solution)/shard_map/all_to_all | solution.py:71
  115.3 0.0 reduce-scatter.2.cloned.1.call-start
  115.3 4.9 %fusion.54 = f32[32,8192]{1,0:T(8,128)S(1)} fusion(bf16[32,512]{1,0:T(8,128)(2,1)S(1)} %all_to_all.55, bf16[512,8192]{1,0:T(8,128)(2,1)} %param.15), kind=kOutput, calls=%fused_computation.95 | convolution fusion | flops 268435456 | bytes 9469952 | tf_op jit(solution)/shard_map/dot_general | solution.py:140
  120.3 20.8 %all-to-all-done.6 = f32[8,8,8192]{2,1,0:T(8,128)} async-done(((f32[8,8,8192]{2,1,0:T(8,128)}), f32[8,8,8192]{2,1,0:T(8,128)}, u32[]{:S(2)}, u32[]{:S(2)}) %all-to-all-start.6) | async-done | bytes 2097184 | tf_op jit(solution)/shard_map/all_to_all | solution.py:71
  141.0 3.4 %convolution_add_fusion = f32[32,8192]{1,0:T(8,128)} fusion(f32[32,8192]{1,0:T(8,128)S(1)} %fusion.54, f32[8,8,8192]{2,1,0:T(8,128)} %all-to-all-done.6, s32[32]{0:T(128)S(1)} %multiply_add_fusion), kind=kOutput, calls=%fused_computation.3 | convolution fusion | flops 201590784 | bytes 4194432 | tf_op jit(solution)/shard_map/dot_general | solution.py:73
  144.5 0.0 reduce-scatter.2.cloned.1.call-update
  144.5 62.0 %reduce-scatter.2.cloned.1.call-done = f32[32,512]{1,0:T(8,128)} async-done(((f32[32,8192]{1,0:T(8,128)}), f32[32,512]{1,0:T(8,128)}) %reduce-scatter.2.cloned.1.call-update) | async-done | bytes 65552 | tf_op jit(solution)/shard_map/reduce_scatter | solution.py:145
  206.5 1.5 convert_element_type.71
  (15 shorter events, 0.2 us)
Async XLA Ops:
  6.5 36.1 %copy-start = (bf16[8,8,128,128]{3,2,1,0:T(8,128)(2,1)S(1)}, bf16[8,8,128,128]{3,2,1,0:T(8,128)(2,1)}, u32[]{:S(2)}) copy-start(bf16[8,8,128,128]{3,2,1,0:T(8,128)(2,1)} %param.22) | copy-start | bytes 6291460
  6.5 13.3 %copy-start.4 = (s32[8,8]{1,0:T(8,128)S(1)}, s32[8,8]{1,0:T(8,128)}, u32[]{:S(2)}) copy-start(s32[8,8]{1,0:T(8,128)} %param.23) | copy-start | bytes 772
  7.4 19.2 %copy-start.1 = (bf16[32,8192]{1,0:T(8,128)(2,1)S(1)}, bf16[32,8192]{1,0:T(8,128)(2,1)}, u32[]{:S(2)}) copy-start(bf16[32,8192]{1,0:T(8,128)(2,1)} %param.13) | copy-start | bytes 1572868
  10.4 11.8 %all-to-all-start = ((s32[8,1,8]{2,1,0:T(1,128)}), s32[8,1,8]{2,1,0:T(1,128)S(1)}, u32[]{:S(2)}, u32[]{:S(2)}) async-start(s32[8,1,8]{2,1,0:T(1,128)} %bitcast.1), calls=%async_computation | async-start | bytes 8192 | tf_op jit(solution)/shard_map/all_to_all | solution.py:56
  22.2 18.0 %all-to-all-start.1 = ((bf16[8,8,8192]{2,1,0:T(8,128)(2,1)}), bf16[8,8,8192]{2,1,0:T(8,128)(2,1)}, u32[]{:S(2)}, u32[]{:S(2)}) async-start(bf16[8,8,8192]{2,1,0:T(8,128)(2,1)} %fusion), calls=%async_computation.1 | async-start | bytes 2097152 | tf_op jit(solution)/shard_map/all_to_all | solution.py:55
  43.9 6.4 %copy-start.3 = (bf16[2,2,1024]{2,1,0:T(2,128)(2,1)S(1)}, bf16[2,2,1024]{2,1,0:T(2,128)(2,1)}, u32[]{:S(2)}) copy-start(bf16[2,2,1024]{2,1,0:T(2,128)(2,1)} %param.18) | copy-start | bytes 24580
  43.9 23.1 %copy-start.6 = (s32[2]{0:T(128)S(1)}, s32[2]{0:T(128)}, u32[]{:S(2)}) copy-start(s32[2]{0:T(128)} %param.19) | copy-start | bytes 28
  46.6 9.3 %all-to-all-start.2 = ((f32[8,8,512]{2,1,0:T(8,128)}), f32[8,8,512]{2,1,0:T(8,128)S(1)}, u32[]{:S(2)}, u32[]{:S(2)}) async-start(f32[8,8,512]{2,1,0:T(8,128)} %reshape_reshape.13), calls=%async_computation.2 | async-start | bytes 262144 | tf_op jit(solution)/shard_map/all_to_all | solution.py:71
  56.7 17.6 %all-to-all-start.3 = ((bf16[16,2,512]{2,1,0:T(2,128)(2,1)}), bf16[16,2,512]{2,1,0:T(2,128)(2,1)S(1)}, u32[]{:S(2)}, u32[]{:S(2)}) async-start(bf16[16,2,512]{2,1,0:T(2,128)(2,1)} %all_to_all.49), calls=%async_computation.3 | async-start | bytes 65536 | tf_op jit(solution)/shard_map/all_to_all | solution.py:137
  74.5 3.9 %copy-start.2 = (bf16[2,8,1024,128]{3,2,1,0:T(8,128)(2,1)S(1)}, bf16[2,8,1024,128]{3,2,1,0:T(8,128)(2,1)}, u32[]{:S(2)}) copy-start(bf16[2,8,1024,128]{3,2,1,0:T(8,128)(2,1)} %param.17) | copy-start | bytes 12582916
  78.4 5.1 %copy-start.5 = (s32[8,8]{1,0:T(8,128)S(1)}, s32[8,8]{1,0:T(8,128)}, u32[]{:S(2)}) copy-start(s32[8,8]{1,0:T(8,128)} %param.25) | copy-start | bytes 772
  79.8 11.1 %all-to-all-start.4 = ((bf16[2,16,512]{2,0,1:T(2,128)(2,1)}), bf16[2,16,512]{2,0,1:T(2,128)(2,1)S(1)}, u32[]{:S(2)}, u32[]{:S(2)}) async-start(bf16[2,16,512]{2,0,1:T(2,128)(2,1)} %copy.28), calls=%async_computation.4 | async-start | bytes 65536 | tf_op jit(solution)/shard_map/all_to_all | solution.py:139
  91.8 8.7 %all-to-all-start.5 = ((bf16[8,8,512]{2,1,0:T(8,128)(2,1)}), bf16[8,8,512]{2,1,0:T(8,128)(2,1)S(1)}, u32[]{:S(2)}, u32[]{:S(2)}) async-start(bf16[8,8,512]{2,1,0:T(8,128)(2,1)} %fusion.17), calls=%async_computation.5 | async-start | bytes 131072 | tf_op jit(solution)/shard_map/all_to_all | solution.py:55
  110.9 30.1 %all-to-all-start.6 = ((f32[8,8,8192]{2,1,0:T(8,128)}), f32[8,8,8192]{2,1,0:T(8,128)}, u32[]{:S(2)}, u32[]{:S(2)}) async-start(f32[8,8,8192]{2,1,0:T(8,128)} %reshape_reshape.15), calls=%async_computation.6 | async-start | bytes 4194304 | tf_op jit(solution)/shard_map/all_to_all | solution.py:71
  115.3 91.2 %reduce-scatter.2.cloned.1.call-start = ((), (), s32[]{:S(2)}) async-start(), calls=%async_computation.8 | async-start | bytes 1114112 | tf_op jit(solution)/shard_map/reduce_scatter | solution.py:145
Sparse Core Ops, SparseCore 0:
  144.6 61.8 reduce-scatter.1
where the time goes:
time: 217 us; the launch traced here: 215 us
  waiting for transfers between devices  118 us (54%)
  starting transfers between devices  36.7 us (17%)
  matrix products  33.2 us (15%)
  between operations  13.6 us (6%)
  local copies, waits for them, and re-layouts  9.21 us (4%)
  other arithmetic  4.36 us (2%)
    reduce_scatter x1, waiting for transfers between devices, body(): lax.psum_scatter(partial_terms, 'tensor', scatter_dimension=1, tiled=True)  62 us
    all_to_all x2, waiting for transfers between devices, return_home(): lax.all_to_all(result, 'dp', split_axis=0, concat_axis=0, tiled=True)  26.3 us
    all_to_all x2, waiting for transfers between devices, visit_store(): lax.all_to_all(packed, 'dp', split_axis=0, concat_axis=0, tiled=True)  12.6 us
    all_to_all x1, starting transfers between devices, body(): lax.all_to_all(query_heads, 'tensor', split_axis=0, concat_axis=1, tiled=...  10.3 us
    all_to_all x2, starting transfers between devices, return_home(): lax.all_to_all(result, 'dp', split_axis=0, concat_axis=0, tiled=True)  8.09 us
    all_to_all x2, starting transfers between devices, visit_store(): lax.all_to_all(packed, 'dp', split_axis=0, concat_axis=0, tiled=True)  7.76 us
    all_to_all x1, waiting for transfers between devices, body(): lax.all_to_all(attended, 'tensor', split_axis=1, concat_axis=0, tiled=True)  7.3 us
    all_to_all x1, waiting for transfers between devices, body(): lax.all_to_all(query_heads, 'tensor', split_axis=0, concat_axis=1, tiled=...  7.25 us
  transfers between devices with their start and end apart: 8, of which 8 were waited for; matrix products, arithmetic and copies ran while one was open for 7% of the time, Pallas kernels for 0%

commit v1 on v0

v1 whole, which is shorter than its diff:
```python
import functools

import jax
import jax.numpy as jnp
from jax import lax
from jax.experimental import pallas as pl
from jax.experimental.pallas import tpu as pltpu
from jax.sharding import PartitionSpec as P

F32 = jnp.float32
BF16 = jnp.bfloat16
I32 = jnp.int32
LANES = 128
EVERY = ("dp", "tensor")


def iota(shape, axis):
    return lax.broadcasted_iota(I32, shape, axis)


def dot(a, b, contract=((1,), (0,))):
    return lax.dot_general(a, b, (contract, ((), ())), preferred_element_type=F32)


def pick(mask, value=1.0):
    return jnp.where(mask, value, 0.0)


def pack_kernel(per_store, tenant_ref, slot_ref, rows_ref, out_ref, place_ref):
    group = lax.axis_index("dp")
    count, width = rows_ref.shape
    tenants = slot_ref.shape[1]
    places = out_ref.shape[0]
    capacity = 8
    stores = places // capacity
    chosen = pick(iota((tenants, count), 0) == tenant_ref[...]).astype(BF16)
    table = jnp.broadcast_to(slot_ref[...].astype(F32), (8, tenants)).astype(BF16)
    slot = dot(table, chosen)[0:1].astype(I32)
    store = slot // per_store
    at_store = pick(iota((stores, count), 0) == store)
    earlier = pick(iota((count, count), 0) < iota((count, count), 1)).astype(BF16)
    before = dot(at_store.astype(BF16), earlier)
    rank = jnp.sum(at_store * before, axis=0, keepdims=True).astype(I32)
    placed = iota((places, count), 0) == store * capacity + rank
    one_hot = pick(placed)
    place_ref[...] = one_hot.astype(BF16)
    hot = one_hot.astype(BF16)
    step = 1024
    for start in range(0, width, step):
        block = dot(hot, rows_ref[:, start : start + step])
        out_ref[:, start : start + step] = block.astype(BF16)
    number = iota((1, count), 1) + 1
    lane_of = iota((LANES, count), 0) % (LANES // 2)
    spread = jnp.where(lane_of == group * capacity + rank, number, 0).astype(F32).astype(BF16)
    by_lane = dot(at_store.astype(BF16), spread, ((1,), (1,)))
    wide = jnp.broadcast_to(by_lane[:, None, :], (stores, capacity, LANES))
    out_ref[:, width : width + LANES] = wide.reshape(places, LANES).astype(BF16)
    slot_col = jnp.sum(jnp.where(placed, slot + 1, 0).astype(F32), axis=1, keepdims=True)
    row_col = jnp.sum(jnp.where(placed, number, 0).astype(F32), axis=1, keepdims=True)
    lane = iota((places, LANES), 1)
    facts = jnp.where(lane == 0, slot_col, jnp.where(lane == 1, row_col, 0.0))
    out_ref[:, width + LANES : width + 2 * LANES] = facts.astype(BF16)


def pack_rows(row_tenant, tenant_slot, rows, places, per_store):
    count, width = rows.shape
    return pl.pallas_call(
        functools.partial(pack_kernel, per_store),
        out_shape=(
            jax.ShapeDtypeStruct((places, width + 2 * LANES), BF16),
            jax.ShapeDtypeStruct((places, count), BF16),
        ),
        compiler_params=pltpu.CompilerParams(vmem_limit_bytes=8 << 20),
        name="pack_rows",
    )(row_tenant.reshape(1, count), tenant_slot.reshape(1, -1), rows)


def query_kernel(where_ref, arrived_ref, tiles_ref, base_ref, out_ref, facts_ref, total):
    me = lax.axis_index("dp")
    slots, per_slot, tile = tiles_ref.shape[:3]
    places = arrived_ref.shape[0]
    width = arrived_ref.shape[1] - 2 * LANES
    blocks = total.shape[1] // tile
    group_rows = base_ref.shape[0] // blocks
    groups = out_ref.shape[0] // base_ref.shape[0]
    capacity = places // groups
    facts = arrived_ref[:, width + LANES : width + 2 * LANES].astype(F32)
    facts_ref[...] = facts
    own_slot = facts[:, 0:1].astype(I32) - 1 - me * slots
    total[...] = jnp.zeros_like(total)
    for t in range(slots):
        mine = own_slot == t
        for k in range(per_slot):
            place = where_ref[t, k]
            source = pl.multiple_of((place // blocks) * tile, tile)
            target = pl.multiple_of((place % blocks) * tile, tile)
            product = dot(arrived_ref[:, pl.ds(source, tile)], tiles_ref[t, k])
            total[:, pl.ds(target, tile)] += jnp.where(mine, product, 0.0)
    stacked = jnp.concatenate(
        [total[:, b * tile : (b + 1) * tile] for b in range(blocks)], axis=0
    ).astype(BF16)
    by_lane = arrived_ref[:, width : width + LANES].astype(F32)
    by_lane = jnp.sum(by_lane.reshape(groups, capacity, LANES), axis=0)[0:1].astype(I32)
    lane = iota((1, LANES), 1)
    home = (lane % places) // capacity * group_rows + by_lane - 1
    home = jnp.where(by_lane > 0, home * blocks + lane // places, -blocks)
    block_rows = group_rows * blocks
    for g in range(groups):
        row = iota((block_rows, LANES), 0) + g * block_rows
        expand = jnp.concatenate(
            [pick(row == home + b).astype(BF16) for b in range(0, blocks, LANES // places)],
            axis=1,
        )
        sent = dot(expand, stacked) + jnp.where(me == g, base_ref[...], 0.0)
        out_ref[g * block_rows : (g + 1) * block_rows, :] = sent.astype(BF16)


def query_visit(arrived, tiles, where, base, groups):
    places = arrived.shape[0]
    slots, per_slot, tile = tiles.shape[:3]
    columns = base.shape[1]
    blocks = columns // tile
    stacked = base.reshape(base.shape[0] * blocks, tile)
    vmem = pl.BlockSpec(memory_space=pltpu.VMEM)
    return pl.pallas_call(
        query_kernel,
        out_shape=(
            jax.ShapeDtypeStruct((groups * stacked.shape[0], tile), BF16),
            jax.ShapeDtypeStruct((places, LANES), F32),
        ),
        in_specs=[pl.BlockSpec(memory_space=pltpu.SMEM), vmem, vmem, vmem],
        scratch_shapes=[pltpu.VMEM((places, columns), F32)],
        compiler_params=pltpu.CompilerParams(vmem_limit_bytes=12 << 20),
        name="query_visit",
    )(where, arrived, tiles, stacked)


def attend_kernel(
    length_ref, arrived_ref, fresh_ref, key_ref, value_ref, out_ref, keys, values, key_sem, value_sem
):
    requests, kv_heads, context, size = key_ref.shape
    for i in range(requests):
        pltpu.make_async_copy(key_ref.at[i], keys.at[i], key_sem.at[i]).start()
    for i in range(requests):
        pltpu.make_async_copy(value_ref.at[i], values.at[i], value_sem.at[i]).start()
    shards = out_ref.shape[1]
    stores = arrived_ref.shape[0]
    scale = size ** (-0.5)
    query = arrived_ref[0].astype(F32)
    for s in range(1, stores):
        query = query + arrived_ref[s].astype(F32)
    fresh = fresh_ref[...].astype(F32)
    upper = iota((8, size), 0) < 4
    position = iota((1, context), 1)
    mixed = [[None] * kv_heads for _ in range(requests)]
    for i in range(requests):
        pltpu.make_async_copy(key_ref.at[i], keys.at[i], key_sem.at[i]).wait()
        visible = position < length_ref[i]
        parts = []
        for g in range(kv_heads):
            first, second = query[2 * g], query[2 * g + 1]
            if i == 0:
                heads = jnp.where(upper, first, pltpu.roll(second, 4, 0))
            else:
                heads = jnp.where(upper, pltpu.roll(first, 4, 0), second)
            heads = heads.astype(BF16)
            scores = dot(heads, keys[i, g], ((1,), (1,))) * scale
            fresh_key = fresh[i, 0:1, g * size : (g + 1) * size]
            own = jnp.sum(heads.astype(F32) * fresh_key, axis=1, keepdims=True) * scale
            scores = jnp.where(visible, scores, -1e30)
            highest = jnp.maximum(jnp.max(scores, axis=1, keepdims=True), own)
            weights = jnp.where(visible, jnp.exp(scores - highest), 0.0)
            own_weight = jnp.exp(own - highest)
            total = jnp.sum(weights, axis=1, keepdims=True) + own_weight
            share = (weights / total).astype(BF16)
            own_share = (own_weight / total).astype(BF16).astype(F32)
            parts.append((share, own_share))
        pltpu.make_async_copy(value_ref.at[i], values.at[i], value_sem.at[i]).wait()
        for g in range(kv_heads):
            share, own_share = parts[g]
            fresh_value = fresh[i, 1:2, g * size : (g + 1) * size]
            mixed[i][g] = dot(share, values[i, g]) + own_share * fresh_value
    for g in range(kv_heads):
        one, two = mixed[0][g], mixed[1][g]
        first = jnp.where(upper, one, pltpu.roll(two, 4, 0)).astype(BF16)
        second = jnp.where(upper, pltpu.roll(one, 4, 0), two).astype(BF16)
        for d in range(out_ref.shape[0]):
            out_ref[d, 2 * g] = first
            out_ref[d, 2 * g + 1] = second


def attend(arrived, keys, values, fresh, lengths, groups):
    requests, kv_heads, context, size = keys.shape
    shards = arrived.shape[0] // (groups * 8)
    vmem = pl.BlockSpec(memory_space=pltpu.VMEM)
    hbm = pl.BlockSpec(memory_space=pl.ANY)
    return pl.pallas_call(
        attend_kernel,
        out_shape=jax.ShapeDtypeStruct((groups, shards, 8, size), BF16),
        in_specs=[pl.BlockSpec(memory_space=pltpu.SMEM), vmem, vmem, hbm, hbm],
        scratch_shapes=[
            pltpu.VMEM(keys.shape, BF16),
            pltpu.VMEM(values.shape, BF16),
            pltpu.SemaphoreType.DMA((requests,)),
            pltpu.SemaphoreType.DMA((requests,)),
        ],
        compiler_params=pltpu.CompilerParams(vmem_limit_bytes=24 << 20),
        name="attend",
    )(lengths, arrived.reshape(groups, shards, 8, size), fresh, keys, values)


def output_kernel(
    where_ref, arrived_ref, facts_ref, tiles_ref, weight_ref, out_ref, weight, rows, total, sems
):
    me = lax.axis_index("dp")
    slots, per_slot, tile = tiles_ref.shape[:3]
    groups, shards, capacity, columns = out_ref.shape
    places = groups * capacity
    depth, width = weight_ref.shape
    chunks = sems.shape[0]
    chunk = width // chunks

    def fetch(c):
        span = pl.ds(c * chunk, chunk)
        return pltpu.make_async_copy(weight_ref.at[:, span], weight.at[:, span], sems.at[c])

    for c in range(chunks):
        fetch(c).start()
    blocks = depth // tile
    group_rows = arrived_ref.shape[0] // (groups * blocks)
    facts = facts_ref[...].astype(I32)
    own_slot = facts[:, 0:1] - 1 - me * slots
    number = facts[:, 1:2]
    home = iota((places, 1), 0) // capacity * group_rows + number - 1
    home = jnp.where(number > 0, home * blocks, -blocks)
    lane = iota((places, arrived_ref.shape[0]), 1)
    for b in range(blocks):
        gather = pick(lane == home + b).astype(BF16)
        rows[:, b * tile : (b + 1) * tile] = dot(gather, arrived_ref[...]).astype(BF16)
    total[...] = jnp.zeros_like(total)
    targets = width // tile
    for t in range(slots):
        mine = own_slot == t
        for k in range(per_slot):
            place = where_ref[t, k]
            source = pl.multiple_of((place // targets) * tile, tile)
            target = pl.multiple_of((place % targets) * tile, tile)
            product = dot(rows[:, pl.ds(source, tile)], tiles_ref[t, k])
            total[:, pl.ds(target, tile)] += jnp.where(mine, product, 0.0)
    per_chunk = chunk // columns
    for c in range(chunks):
        fetch(c).wait()
        for n in range(per_chunk):
            shard = c * per_chunk + n
            span = slice(shard * columns, (shard + 1) * columns)
            result = dot(rows[...], weight[:, span]) + total[:, span]
            out_ref[:, shard] = result.reshape(groups, capacity, columns).astype(BF16)


def output_visit(arrived, facts, tiles, where, weight, groups):
    depth, width = weight.shape
    places = facts.shape[0]
    shards = width // depth
    chunks = 8
    vmem = pl.BlockSpec(memory_space=pltpu.VMEM)
    return pl.pallas_call(
        output_kernel,
        out_shape=jax.ShapeDtypeStruct((groups, shards, places // groups, depth), BF16),
        in_specs=[
            pl.BlockSpec(memory_space=pltpu.SMEM),
            vmem,
            vmem,
            vmem,
            pl.BlockSpec(memory_space=pl.ANY),
        ],
        scratch_shapes=[
            pltpu.VMEM((depth, width), BF16),
            pltpu.VMEM((places, depth), BF16),
            pltpu.VMEM((places, width), F32),
            pltpu.SemaphoreType.DMA((chunks,)),
        ],
        compiler_params=pltpu.CompilerParams(vmem_limit_bytes=24 << 20),
        name="output_visit",
    )(where, arrived, facts, tiles, weight)


def finish_kernel(arrived_ref, place_ref, out_ref):
    stores, shards, capacity, columns = arrived_ref.shape
    total = arrived_ref[:, 0].astype(F32)
    for j in range(1, shards):
        total = total + arrived_ref[:, j].astype(F32)
    rounded = total.reshape(stores * capacity, columns).astype(BF16)
    out_ref[...] = dot(place_ref[...], rounded, ((0,), (0,))).astype(BF16)


def finish(arrived, place):
    return pl.pallas_call(
        finish_kernel,
        out_shape=jax.ShapeDtypeStruct((place.shape[1], arrived.shape[3]), BF16),
        compiler_params=pltpu.CompilerParams(vmem_limit_bytes=8 << 20),
        name="finish",
    )(arrived, place)


def swap(blocks, axes):
    return lax.all_to_all(blocks, axes, split_axis=0, concat_axis=0, tiled=True)


def body(
    activations,
    query_weight,
    output_weight,
    key_cache,
    value_cache,
    fresh_pair,
    cache_length,
    row_tenant,
    tenant_slot,
    query_deltas,
    query_where,
    output_deltas,
    output_where,
):
    groups = lax.axis_size("dp")
    shards = lax.axis_size("tensor")
    per_store = query_deltas.shape[0]
    capacity = 8
    packed, place = pack_rows(row_tenant, tenant_slot, activations, groups * capacity, per_store)
    arrived = swap(packed, "dp")
    base_query = jnp.dot(activations, query_weight, preferred_element_type=F32)
    sent_query, facts = query_visit(arrived, query_deltas, query_where, base_query, groups)
    query = swap(sent_query, EVERY)
    attended = attend(query, key_cache, value_cache, fresh_pair, cache_length, groups)
    size = attended.shape[3]
    rows = swap(attended.reshape(-1, size), EVERY)
    parts = output_visit(rows, facts, output_deltas, output_where, output_weight, groups)
    columns = parts.shape[3]
    summed = swap(parts.reshape(-1, columns), EVERY)
    return finish(summed.reshape(groups, shards, capacity, columns), place)


def solution(mesh):
    placed = (
        P("dp", None),
        P(None, "tensor"),
        P("tensor", None),
        P(("dp", "tensor"), None, None, None),
        P(("dp", "tensor"), None, None, None),
        P(("dp", "tensor"), None, None),
        P(("dp", "tensor")),
        P("dp"),
        P(),
        P("dp", "tensor", None, None),
        P("dp", "tensor"),
        P("dp", "tensor", None, None),
        P("dp", "tensor"),
    )
    return jax.shard_map(
        body, mesh=mesh, in_specs=placed, out_specs=P("dp", "tensor"), check_vma=False
    )
```

time: 217 us -> 103 us (0.47)
  waiting for transfers between devices: 118 us -> 9.97 us
  blocking collectives: 0 us -> 57 us
  starting transfers between devices: 36.7 us -> 6.86 us
  matrix products: 33.2 us -> 5.2 us
  between operations: 13.6 us -> 0.07 us
  Pallas kernels: 0 us -> 13.2 us
  other arithmetic: 4.36 us -> 0 us
    reduce_scatter x1 -> x0, waiting for transfers between devices: 62 us -> none  [body(): lax.psum_scatter(partial_terms, 'tensor', scatter_dimension=1, tiled=True)]
    all_to_all x0 -> x3, blocking collectives: none -> 57 us  [swap(): return lax.all_to_all(blocks, axes, split_axis=0, concat_axis=0, tiled=True)]
    all_to_all x7 -> x1, waiting for transfers between devices: 55.7 us -> 9.97 us  [swap(): return lax.all_to_all(blocks, axes, split_axis=0, concat_axis=0, tiled=True)]
    all_to_all x7 -> x1, starting transfers between devices: 36.7 us -> 6.86 us  [swap(): return lax.all_to_all(blocks, axes, split_axis=0, concat_axis=0, tiled=True)]
    dot_general x15 -> x1, matrix products: 33.2 us -> 5.2 us  [body(): base_query = jnp.dot(activations, query_weight, preferred_element_type=F32)]
    pallas_call x0 -> x5, Pallas kernels: none -> 13.2 us  [the longest x1 5.37 us: output_visit(): pl.pallas_call(output_kernel, out_shape=jax.ShapeDtypeStruct((groups, sha...]
    unnamed x15 -> x24, local copies, waits for them, and re-layouts: 1.52 us -> 10.1 us
    another operation x3 -> x0, local copies, waits for them, and re-layouts: 3.45 us -> none  [the longest x2 3.43 us: visit_store(): return result.reshape(stores, capacity, out_columns)]
  transfers between devices with their start and end apart: 8 -> 1, of which waited for: 8 -> 1; matrix products, arithmetic and copies ran while one was open for 7% -> 5% of each run, Pallas kernels for 0% -> 0%
where the time goes in v1:
time: 103 us; the launch traced here: 102 us
  blocking collectives  57 us (55%)
  Pallas kernels  13.2 us (13%)
  local copies, waits for them, and re-layouts  10.2 us (10%)
  waiting for transfers between devices  9.97 us (10%)
  starting transfers between devices  6.86 us (7%)
  matrix products  5.2 us (5%)
    all_to_all x3, blocking collectives, swap(): return lax.all_to_all(blocks, axes, split_axis=0, concat_axis=0, tiled=True)  57 us
    unnamed x24, local copies, waits for them, and re-layouts  10.1 us
    all_to_all x1, waiting for transfers between devices, swap(): return lax.all_to_all(blocks, axes, split_axis=0, concat_axis=0, tiled=True)  9.97 us
    all_to_all x1, starting transfers between devices, swap(): return lax.all_to_all(blocks, axes, split_axis=0, concat_axis=0, tiled=True)  6.86 us
    pallas_call x1, Pallas kernels, output_visit(): pl.pallas_call(output_kernel, out_shape=jax.ShapeDtypeStruct((groups, sha...  5.37 us
    dot_general x1, matrix products, body(): base_query = jnp.dot(activations, query_weight, preferred_element_type=F32)  5.2 us
    pallas_call x1, Pallas kernels, attend(): pl.pallas_call(attend_kernel, out_shape=jax.ShapeDtypeStruct((groups, sha...  3.66 us
  transfers between devices with their start and end apart: 1, of which 1 were waited for; matrix products, arithmetic and copies ran while one was open for 5% of the time, Pallas kernels for 0%

profile of v1, /device:TPU:1, one launch (start us, length us, event | category | flops | bytes accessed | tf_op | source)
XLA Modules:
  0.0 102.5 jit_solution(10307026380614551580)
XLA Ops:
  0.0 0.0 copy-start.1
  0.0 1.0 %copy-done.1 = bf16[32,8192]{1,0:T(8,128)(2,1)S(1)} copy-done((bf16[32,8192]{1,0:T(8,128)(2,1)S(1)}, bf16[32,8192]{1,0:T(8,128)(2,1)}, u32[]{:S(2)}) %copy-start.1) | copy-done | bytes 524312
  1.0 0.0 copy-start.9
  1.0 0.7 copy-done.9
  1.7 0.0 copy-start.10
  1.7 0.7 copy-done.10
  2.4 1.7 %pack_rows.1 = (bf16[64,8448]{1,0:T(8,128)(2,1)}, bf16[64,32]{1,0:T(8,128)(2,1)S(1)}) custom-call(s32[1,32]{1,0:T(1,128)S(1)} %bitcast.19, s32[1,64]{1,0:T(1,128)S(1)} %bitcast.20, bf16[32,8192]{1,0:T(8,128)(2,1)S(1)} %copy-done.1), custom_call_target="tpu_custom_call" | custom-call | tf_op jit(solution)/shard_map/pack_rows/pallas_call | solution.py:67
  4.0 6.9 %all-to-all-start = ((bf16[8,8,8448]{2,1,0:T(8,128)(2,1)}), bf16[8,8,8448]{2,1,0:T(8,128)(2,1)S(1)}, u32[]{:S(2)}, u32[]{:S(2)}) async-start(bf16[8,8,8448]{2,1,0:T(8,128)(2,1)} %bitcast.2), calls=%async_computation | async-start | bytes 2162688 | tf_op jit(solution)/shard_map/all_to_all | solution.py:306
  10.9 0.0 copy-start.4
  10.9 0.0 copy-start.7
  10.9 0.0 copy-start.6
  10.9 0.0 copy-start.11
  10.9 5.2 %fusion = f32[32,512]{1,0:T(8,128)S(1)} fusion(bf16[32,8192]{1,0:T(8,128)(2,1)} %rows_ref.1, bf16[8192,512]{1,0:T(8,128)(2,1)} %param.14), kind=kOutput, calls=%fused_computation | convolution fusion | flops 268435456 | bytes 8978432 | tf_op jit(solution)/shard_map/dot_general | solution.py:330
  16.2 10.0 %all-to-all-done = bf16[8,8,8448]{2,1,0:T(8,128)(2,1)S(1)} async-done(((bf16[8,8,8448]{2,1,0:T(8,128)(2,1)}), bf16[8,8,8448]{2,1,0:T(8,128)(2,1)S(1)}, u32[]{:S(2)}, u32[]{:S(2)}) %all-to-all-start) | async-done | bytes 1081376 | tf_op jit(solution)/shard_map/all_to_all | solution.py:306
  26.1 0.0 copy-done.4
  26.1 0.0 copy-done.7
  26.1 1.7 %query_visit.1 = (bf16[1024,128]{1,0:T(8,128)(2,1)S(1)}, f32[64,128]{1,0:T(8,128)S(1)}) custom-call(s32[8,8]{1,0:T(8,128)S(1)} %copy-done.7, bf16[64,8448]{1,0:T(8,128)(2,1)S(1)} %bitcast.12, bf16[8,8,128,128]{3,2,1,0:T(8,128)(2,1)S(1)} %copy-done.4, f32[128,128]{1,0:T(8,128)S(1)} %reshape.31.base_ref), custom_call_target="tpu_custom_call" | custom-call | tf_op jit(solution)/shard_map/query_visit/pallas_call | solution.py:125
  27.8 19.1 %all_to_all.40 = bf16[128,8,128]{2,1,0:T(8,128)(2,1)S(1)} all-to-all(bf16[128,8,128]{2,1,0:T(8,128)(2,1)S(1)} %bitcast.18), channel_id=1, replica_groups=mesh['dp'=8,'tensor'=16] {'dp','tensor'}, dimensions={0} | all-to-all | bytes 524288 | tf_op jit(solution)/shard_map/all_to_all | solution.py:306
  46.9 0.0 copy-done.6
  46.9 0.0 copy-done.11
  46.9 0.0 copy-start.2
  46.9 2.2 %copy-done.2 = bf16[2,8,1024,128]{3,2,1,0:T(8,128)(2,1)S(1)} copy-done((bf16[2,8,1024,128]{3,2,1,0:T(8,128)(2,1)S(1)}, bf16[2,8,1024,128]{3,2,1,0:T(8,128)(2,1)}, u32[]{:S(2)}) %copy-start.2) | copy-done | bytes 4194328
  49.1 0.0 copy-start.3
  49.1 2.2 %copy-done.3 = bf16[2,8,1024,128]{3,2,1,0:T(8,128)(2,1)S(1)} copy-done((bf16[2,8,1024,128]{3,2,1,0:T(8,128)(2,1)S(1)}, bf16[2,8,1024,128]{3,2,1,0:T(8,128)(2,1)}, u32[]{:S(2)}) %copy-start.3) | copy-done | bytes 4194328
  51.3 0.0 copy-start.5
  51.3 0.0 copy-start.8
  51.3 3.7 %attend.1 = bf16[8,16,8,128]{3,2,1,0:T(8,128)(2,1)S(1)} custom-call(s32[2]{0:T(128)S(1)} %copy-done.11, bf16[8,16,8,128]{3,2,1,0:T(8,128)(2,1)S(1)} %bitcast.16, bf16[2,2,1024]{2,1,0:T(2,128)(2,1)S(1)} %copy-done.6, bf16[2,8,1024,128]{3,2,1,0:T(8,128)(2,1)S(1)} %copy-done.2, bf16[2,8,1024,128]{3,2,1,0:T(8,128)(2,1)S(1)} %copy-done.3), custom_call_target="tpu_custom_call" | custom-call | tf_op jit(solution)/shard_map/attend/pallas_call | solution.py:197
  54.9 15.0 %all_to_all.41 = bf16[128,8,128]{2,1,0:T(8,128)(2,1)S(1)} all-to-all(bf16[128,8,128]{2,1,0:T(8,128)(2,1)S(1)} %bitcast.17), channel_id=1, replica_groups=mesh['dp'=8,'tensor'=16] {'dp','tensor'}, dimensions={0} | all-to-all | bytes 524288 | tf_op jit(solution)/shard_map/all_to_all | solution.py:306
  69.9 0.0 copy-done.5
  69.9 0.0 copy-done.8
  69.9 0.0 copy-start
  69.9 3.4 %copy-done = bf16[512,8192]{1,0:T(8,128)(2,1)S(1)} copy-done((bf16[512,8192]{1,0:T(8,128)(2,1)S(1)}, bf16[512,8192]{1,0:T(8,128)(2,1)}, u32[]{:S(2)}) %copy-start) | copy-done | bytes 8388632
  73.3 5.4 %output_visit.1 = bf16[8,16,8,512]{3,2,1,0:T(8,128)(2,1)S(1)} custom-call(s32[8,8]{1,0:T(8,128)S(1)} %copy-done.8, bf16[1024,128]{1,0:T(8,128)(2,1)S(1)} %bitcast.15, f32[64,128]{1,0:T(8,128)S(1)} %get-tuple-element.11.facts_ref, bf16[8,8,128,128]{3,2,1,0:T(8,128)(2,1)S(1)} %copy-done.5, bf16[512,8192]{1,0:T(8,128)(2,1)S(1)} %copy-done), custom_call_target="tpu_custom_call" | custom-call | tf_op jit(solution)/shard_map/output_visit/pallas_call | solution.py:266
  78.7 22.9 %all_to_all.42 = bf16[128,8,512]{2,1,0:T(8,128)(2,1)S(1)} all-to-all(bf16[128,8,512]{2,1,0:T(8,128)(2,1)S(1)} %bitcast.14), channel_id=1, replica_groups=mesh['dp'=8,'tensor'=16] {'dp','tensor'}, dimensions={0} | all-to-all | bytes 2097152 | tf_op jit(solution)/shard_map/all_to_all | solution.py:306
  101.6 0.9 finish.1
  (1 shorter events, 0.0 us)
Async XLA Ops:
  0.0 1.0 %copy-start.1 = (bf16[32,8192]{1,0:T(8,128)(2,1)S(1)}, bf16[32,8192]{1,0:T(8,128)(2,1)}, u32[]{:S(2)}) copy-start(bf16[32,8192]{1,0:T(8,128)(2,1)} %rows_ref.1) | copy-start | bytes 1572868
  1.0 0.7 copy-start.9
  1.7 0.7 copy-start.10
  4.0 22.1 %all-to-all-start = ((bf16[8,8,8448]{2,1,0:T(8,128)(2,1)}), bf16[8,8,8448]{2,1,0:T(8,128)(2,1)S(1)}, u32[]{:S(2)}, u32[]{:S(2)}) async-start(bf16[8,8,8448]{2,1,0:T(8,128)(2,1)} %bitcast.2), calls=%async_computation | async-start | bytes 2162688 | tf_op jit(solution)/shard_map/all_to_all | solution.py:306
  10.9 15.2 %copy-start.4 = (bf16[8,8,128,128]{3,2,1,0:T(8,128)(2,1)S(1)}, bf16[8,8,128,128]{3,2,1,0:T(8,128)(2,1)}, u32[]{:S(2)}) copy-start(bf16[8,8,128,128]{3,2,1,0:T(8,128)(2,1)} %tiles_ref.2) | copy-start | bytes 6291460
  10.9 15.2 %copy-start.7 = (s32[8,8]{1,0:T(8,128)S(1)}, s32[8,8]{1,0:T(8,128)}, u32[]{:S(2)}) copy-start(s32[8,8]{1,0:T(8,128)} %where_ref.2) | copy-start | bytes 772
  10.9 36.0 %copy-start.6 = (bf16[2,2,1024]{2,1,0:T(2,128)(2,1)S(1)}, bf16[2,2,1024]{2,1,0:T(2,128)(2,1)}, u32[]{:S(2)}) copy-start(bf16[2,2,1024]{2,1,0:T(2,128)(2,1)} %fresh_ref.1) | copy-start | bytes 24580
  10.9 36.0 %copy-start.11 = (s32[2]{0:T(128)S(1)}, s32[2]{0:T(128)}, u32[]{:S(2)}) copy-start(s32[2]{0:T(128)} %length_ref.1) | copy-start | bytes 28
  46.9 2.2 %copy-start.2 = (bf16[2,8,1024,128]{3,2,1,0:T(8,128)(2,1)S(1)}, bf16[2,8,1024,128]{3,2,1,0:T(8,128)(2,1)}, u32[]{:S(2)}) copy-start(bf16[2,8,1024,128]{3,2,1,0:T(8,128)(2,1)} %key_ref.1) | copy-start | bytes 12582916
  49.1 2.2 %copy-start.3 = (bf16[2,8,1024,128]{3,2,1,0:T(8,128)(2,1)S(1)}, bf16[2,8,1024,128]{3,2,1,0:T(8,128)(2,1)}, u32[]{:S(2)}) copy-start(bf16[2,8,1024,128]{3,2,1,0:T(8,128)(2,1)} %value_ref.1) | copy-start | bytes 12582916
  51.3 18.6 %copy-start.5 = (bf16[8,8,128,128]{3,2,1,0:T(8,128)(2,1)S(1)}, bf16[8,8,128,128]{3,2,1,0:T(8,128)(2,1)}, u32[]{:S(2)}) copy-start(bf16[8,8,128,128]{3,2,1,0:T(8,128)(2,1)} %tiles_ref.3) | copy-start | bytes 6291460
  51.3 18.6 %copy-start.8 = (s32[8,8]{1,0:T(8,128)S(1)}, s32[8,8]{1,0:T(8,128)}, u32[]{:S(2)}) copy-start(s32[8,8]{1,0:T(8,128)} %where_ref.3) | copy-start | bytes 772
  69.9 3.4 %copy-start = (bf16[512,8192]{1,0:T(8,128)(2,1)S(1)}, bf16[512,8192]{1,0:T(8,128)(2,1)}, u32[]{:S(2)}) copy-start(bf16[512,8192]{1,0:T(8,128)(2,1)} %weight_ref.1) | copy-start | bytes 25165828

commit v2 on v1

--- a/solution.py
+++ b/solution.py
@@ -12,6 +12,7 @@
 I32 = jnp.int32
 LANES = 128
 EVERY = ("dp", "tensor")
+COST = pl.CostEstimate(flops=1 << 35, bytes_accessed=48 << 20, transcendentals=0)
 
 
 def iota(shape, axis):
@@ -130,19 +131,16 @@
         ),
         in_specs=[pl.BlockSpec(memory_space=pltpu.SMEM), vmem, vmem, vmem],
         scratch_shapes=[pltpu.VMEM((places, columns), F32)],
+        cost_estimate=COST,
         compiler_params=pltpu.CompilerParams(vmem_limit_bytes=12 << 20),
         name="query_visit",
     )(where, arrived, tiles, stacked)
 
 
 def attend_kernel(
-    length_ref, arrived_ref, fresh_ref, key_ref, value_ref, out_ref, keys, values, key_sem, value_sem
+    length_ref, arrived_ref, fresh_ref, keys, values, out_ref
 ):
-    requests, kv_heads, context, size = key_ref.shape
-    for i in range(requests):
-        pltpu.make_async_copy(key_ref.at[i], keys.at[i], key_sem.at[i]).start()
-    for i in range(requests):
-        pltpu.make_async_copy(value_ref.at[i], values.at[i], value_sem.at[i]).start()
+    requests, kv_heads, context, size = keys.shape
     shards = out_ref.shape[1]
     stores = arrived_ref.shape[0]
     scale = size ** (-0.5)
@@ -154,7 +152,6 @@
     position = iota((1, context), 1)
     mixed = [[None] * kv_heads for _ in range(requests)]
     for i in range(requests):
-        pltpu.make_async_copy(key_ref.at[i], keys.at[i], key_sem.at[i]).wait()
         visible = position < length_ref[i]
         parts = []
         for g in range(kv_heads):
@@ -175,7 +172,6 @@
             share = (weights / total).astype(BF16)
             own_share = (own_weight / total).astype(BF16).astype(F32)
             parts.append((share, own_share))
-        pltpu.make_async_copy(value_ref.at[i], values.at[i], value_sem.at[i]).wait()
         for g in range(kv_heads):
             share, own_share = parts[g]
             fresh_value = fresh[i, 1:2, g * size : (g + 1) * size]
@@ -193,39 +189,24 @@
     requests, kv_heads, context, size = keys.shape
     shards = arrived.shape[0] // (groups * 8)
     vmem = pl.BlockSpec(memory_space=pltpu.VMEM)
-    hbm = pl.BlockSpec(memory_space=pl.ANY)
     return pl.pallas_call(
         attend_kernel,
         out_shape=jax.ShapeDtypeStruct((groups, shards, 8, size), BF16),
-        in_specs=[pl.BlockSpec(memory_space=pltpu.SMEM), vmem, vmem, hbm, hbm],
-        scratch_shapes=[
-            pltpu.VMEM(keys.shape, BF16),
-            pltpu.VMEM(values.shape, BF16),
-            pltpu.SemaphoreType.DMA((requests,)),
-            pltpu.SemaphoreType.DMA((requests,)),
-        ],
-        compiler_params=pltpu.CompilerParams(vmem_limit_bytes=24 << 20),
+        in_specs=[pl.BlockSpec(memory_space=pltpu.SMEM), vmem, vmem, vmem, vmem],
+        cost_estimate=COST,
+        compiler_params=pltpu.CompilerParams(vmem_limit_bytes=16 << 20),
         name="attend",
     )(lengths, arrived.reshape(groups, shards, 8, size), fresh, keys, values)
 
 
 def output_kernel(
-    where_ref, arrived_ref, facts_ref, tiles_ref, weight_ref, out_ref, weight, rows, total, sems
+    where_ref, arrived_ref, facts_ref, tiles_ref, weight, out_ref, rows, total
 ):
     me = lax.axis_index("dp")
     slots, per_slot, tile = tiles_ref.shape[:3]
     groups, shards, capacity, columns = out_ref.shape
     places = groups * capacity
-    depth, width = weight_ref.shape
-    chunks = sems.shape[0]
-    chunk = width // chunks
-
-    def fetch(c):
-        span = pl.ds(c * chunk, chunk)
-        return pltpu.make_async_copy(weight_ref.at[:, span], weight.at[:, span], sems.at[c])
-
-    for c in range(chunks):
-        fetch(c).start()
+    depth, width = weight.shape
     blocks = depth // tile
     group_rows = arrived_ref.shape[0] // (groups * blocks)
     facts = facts_ref[...].astype(I32)
@@ -247,21 +228,16 @@
             target = pl.multiple_of((place % targets) * tile, tile)
             product = dot(rows[:, pl.ds(source, tile)], tiles_ref[t, k])
             total[:, pl.ds(target, tile)] += jnp.where(mine, product, 0.0)
-    per_chunk = chunk // columns
-    for c in range(chunks):
-        fetch(c).wait()
-        for n in range(per_chunk):
-            shard = c * per_chunk + n
-            span = slice(shard * columns, (shard + 1) * columns)
-            result = dot(rows[...], weight[:, span]) + total[:, span]
-            out_ref[:, shard] = result.reshape(groups, capacity, columns).astype(BF16)
+    for shard in range(shards):
+        span = slice(shard * columns, (shard + 1) * columns)
+        result = dot(rows[...], weight[:, span]) + total[:, span]
+        out_ref[:, shard] = result.reshape(groups, capacity, columns).astype(BF16)
 
 
 def output_visit(arrived, facts, tiles, where, weight, groups):
     depth, width = weight.shape
     places = facts.shape[0]
     shards = width // depth
-    chunks = 8
     vmem = pl.BlockSpec(memory_space=pltpu.VMEM)
     return pl.pallas_call(
         output_kernel,
@@ -271,15 +247,14 @@
             vmem,
             vmem,
             vmem,
-            pl.BlockSpec(memory_space=pl.ANY),
+            vmem,
         ],
         scratch_shapes=[
-            pltpu.VMEM((depth, width), BF16),
             pltpu.VMEM((places, depth), BF16),
             pltpu.VMEM((places, width), F32),
-            pltpu.SemaphoreType.DMA((chunks,)),
         ],
-        compiler_params=pltpu.CompilerParams(vmem_limit_bytes=24 << 20),
+        cost_estimate=COST,
+        compiler_params=pltpu.CompilerParams(vmem_limit_bytes=20 << 20),
         name="output_visit",
     )(where, arrived, facts, tiles, weight)
 

time: 103 us -> 91.6 us (0.89)
  local copies, waits for them, and re-layouts: 10.2 us -> 2.42 us
  Pallas kernels: 13.2 us -> 9.74 us
    unnamed x24 -> x26, local copies, waits for them, and re-layouts: 10.1 us -> 2.4 us
    pallas_call x1, Pallas kernels: 5.37 us -> 3.15 us  [output_visit(): pl.pallas_call(output_kernel, out_shape=jax.ShapeDtypeStruct((groups, sha...]
    pallas_call x1, Pallas kernels: 3.66 us -> 2.37 us  [attend(): pl.pallas_call(attend_kernel, out_shape=jax.ShapeDtypeStruct((groups, sha...]
  transfers between devices with their start and end apart: 1 -> 1, of which waited for: 1 -> 1; matrix products, arithmetic and copies ran while one was open for 5% -> 6% of each run, Pallas kernels for 0% -> 0%
where the time goes in v2:
time: 91.6 us; the launch traced here: 91.3 us
  blocking collectives  57 us (62%)
  waiting for transfers between devices  9.99 us (11%)
  Pallas kernels  9.74 us (11%)
  starting transfers between devices  6.86 us (7%)
  matrix products  5.2 us (6%)
  local copies, waits for them, and re-layouts  2.42 us (3%)
    all_to_all x3, blocking collectives, swap(): return lax.all_to_all(blocks, axes, split_axis=0, concat_axis=0, tiled=True)  57 us
    all_to_all x1, waiting for transfers between devices, swap(): return lax.all_to_all(blocks, axes, split_axis=0, concat_axis=0, tiled=True)  9.99 us
    all_to_all x1, starting transfers between devices, swap(): return lax.all_to_all(blocks, axes, split_axis=0, concat_axis=0, tiled=True)  6.86 us
    dot_general x1, matrix products, body(): base_query = jnp.dot(activations, query_weight, preferred_element_type=F32)  5.2 us
    pallas_call x1, Pallas kernels, output_visit(): pl.pallas_call(output_kernel, out_shape=jax.ShapeDtypeStruct((groups, sha...  3.15 us
    unnamed x26, local copies, waits for them, and re-layouts  2.4 us
    pallas_call x1, Pallas kernels, attend(): pl.pallas_call(attend_kernel, out_shape=jax.ShapeDtypeStruct((groups, sha...  2.37 us
  transfers between devices with their start and end apart: 1, of which 1 were waited for; matrix products, arithmetic and copies ran while one was open for 6% of the time, Pallas kernels for 0%

profile of v2, /device:TPU:1, one launch (start us, length us, event | category | flops | bytes accessed | tf_op | source)
XLA Modules:
  0.0 91.3 jit_solution(6751214866755168142)
XLA Ops:
  0.0 0.0 copy-start
  0.0 1.0 %copy-done = bf16[32,8192]{1,0:T(8,128)(2,1)S(1)} copy-done((bf16[32,8192]{1,0:T(8,128)(2,1)S(1)}, bf16[32,8192]{1,0:T(8,128)(2,1)}, u32[]{:S(2)}) %copy-start) | copy-done | bytes 524312
  1.0 0.0 copy-start.1
  1.0 0.7 copy-done.1
  1.7 0.0 copy-start.2
  1.7 0.7 copy-done.2
  2.4 1.7 %pack_rows.1 = (bf16[64,8448]{1,0:T(8,128)(2,1)}, bf16[64,32]{1,0:T(8,128)(2,1)S(1)}) custom-call(s32[1,32]{1,0:T(1,128)S(1)} %bitcast.19, s32[1,64]{1,0:T(1,128)S(1)} %bitcast.20, bf16[32,8192]{1,0:T(8,128)(2,1)S(1)} %copy-done), custom_call_target="tpu_custom_call" | custom-call | tf_op jit(solution)/shard_map/pack_rows/pallas_call | solution.py:68
  4.0 6.9 %all-to-all-start = ((bf16[8,8,8448]{2,1,0:T(8,128)(2,1)}), bf16[8,8,8448]{2,1,0:T(8,128)(2,1)S(1)}, u32[]{:S(2)}, u32[]{:S(2)}) async-start(bf16[8,8,8448]{2,1,0:T(8,128)(2,1)} %bitcast.2), calls=%async_computation | async-start | bytes 2162688 | tf_op jit(solution)/shard_map/all_to_all | solution.py:281
  10.9 0.0 copy-start.5
  10.9 0.0 copy-start.8
  10.9 5.2 %fusion = f32[32,512]{1,0:T(8,128)S(1)} fusion(bf16[32,8192]{1,0:T(8,128)(2,1)} %rows_ref.1, bf16[8192,512]{1,0:T(8,128)(2,1)} %param.14), kind=kOutput, calls=%fused_computation | convolution fusion | flops 268435456 | bytes 8978432 | tf_op jit(solution)/shard_map/dot_general | solution.py:305
  16.2 10.0 %all-to-all-done = bf16[8,8,8448]{2,1,0:T(8,128)(2,1)S(1)} async-done(((bf16[8,8,8448]{2,1,0:T(8,128)(2,1)}), bf16[8,8,8448]{2,1,0:T(8,128)(2,1)S(1)}, u32[]{:S(2)}, u32[]{:S(2)}) %all-to-all-start) | async-done | bytes 1081376 | tf_op jit(solution)/shard_map/all_to_all | solution.py:281
  26.1 0.0 copy-done.5
  26.1 0.0 copy-done.8
  26.2 0.0 copy-start.3
  26.2 0.0 copy-start.4
  26.2 0.0 copy-start.7
  26.2 0.0 copy-start.10
  26.2 0.0 slice-start
  26.2 1.7 %query_visit.1 = (bf16[1024,128]{1,0:T(8,128)(2,1)S(1)}, f32[64,128]{1,0:T(8,128)S(1)}) custom-call(s32[8,8]{1,0:T(8,128)S(1)} %copy-done.8, bf16[64,8448]{1,0:T(8,128)(2,1)S(1)} %bitcast.13, bf16[8,8,128,128]{3,2,1,0:T(8,128)(2,1)S(1)} %copy-done.5, f32[128,128]{1,0:T(8,128)S(1)} %reshape.31.base_ref), custom_call_target="tpu_custom_call" | custom-call | flops 34359738368 | bytes 50331648 | tf_op jit(solution)/shard_map/query_visit/pallas_call | solution.py:126
  27.9 19.1 %all_to_all.40 = bf16[128,8,128]{2,1,0:T(8,128)(2,1)S(1)} all-to-all(bf16[128,8,128]{2,1,0:T(8,128)(2,1)S(1)} %bitcast.15), channel_id=1, replica_groups=mesh['dp'=8,'tensor'=16] {'dp','tensor'}, dimensions={0} | all-to-all | bytes 524288 | tf_op jit(solution)/shard_map/all_to_all | solution.py:281
  46.9 0.0 slice-start.1
  46.9 0.0 copy-done.3
  46.9 0.0 copy-done.4
  46.9 0.0 copy-done.7
  46.9 0.0 copy-done.10
  47.0 0.0 copy-start.6
  47.0 0.0 copy-start.9
  47.0 2.4 %attend.1 = bf16[8,16,8,128]{3,2,1,0:T(8,128)(2,1)S(1)} custom-call(s32[2]{0:T(128)S(1)} %copy-done.10, bf16[8,16,8,128]{3,2,1,0:T(8,128)(2,1)S(1)} %bitcast.17, bf16[2,2,1024]{2,1,0:T(2,128)(2,1)S(1)} %copy-done.7, bf16[2,8,1024,128]{3,2,1,0:T(8,128)(2,1)S(1)} %copy-done.3, bf16[2,8,1024,128]{3,2,1,0:T(8,128)(2,1)S(1)} %copy-done.4), custom_call_target="tpu_custom_call" | custom-call | flops 34359738368 | bytes 50331648 | tf_op jit(solution)/shard_map/attend/pallas_call | solution.py:192
  49.4 15.0 %all_to_all.41 = bf16[128,8,128]{2,1,0:T(8,128)(2,1)S(1)} all-to-all(bf16[128,8,128]{2,1,0:T(8,128)(2,1)S(1)} %bitcast.18), channel_id=1, replica_groups=mesh['dp'=8,'tensor'=16] {'dp','tensor'}, dimensions={0} | all-to-all | bytes 524288 | tf_op jit(solution)/shard_map/all_to_all | solution.py:281
  64.3 0.0 slice-done
  64.3 0.0 slice-done.1
  64.3 0.0 copy-done.6
  64.3 0.0 copy-done.9
  64.3 3.1 %output_visit.1 = bf16[8,16,8,512]{3,2,1,0:T(8,128)(2,1)S(1)} custom-call(s32[8,8]{1,0:T(8,128)S(1)} %copy-done.9, bf16[1024,128]{1,0:T(8,128)(2,1)S(1)} %bitcast.16, f32[64,128]{1,0:T(8,128)S(1)} %get-tuple-element.11.facts_ref, bf16[8,8,128,128]{3,2,1,0:T(8,128)(2,1)S(1)} %copy-done.6, bf16[512,8192]{1,0:T(8,128)(2,1)S(1)} %bitcast.22), custom_call_target="tpu_custom_call" | custom-call | flops 34359738368 | bytes 50331648 | tf_op jit(solution)/shard_map/output_visit/pallas_call | solution.py:242
  67.5 22.9 %all_to_all.42 = bf16[128,8,512]{2,1,0:T(8,128)(2,1)S(1)} all-to-all(bf16[128,8,512]{2,1,0:T(8,128)(2,1)S(1)} %bitcast.14), channel_id=1, replica_groups=mesh['dp'=8,'tensor'=16] {'dp','tensor'}, dimensions={0} | all-to-all | bytes 2097152 | tf_op jit(solution)/shard_map/all_to_all | solution.py:281
  90.4 0.9 finish.1
  (2 shorter events, 0.0 us)
Async XLA Ops:
  0.0 1.0 %copy-start = (bf16[32,8192]{1,0:T(8,128)(2,1)S(1)}, bf16[32,8192]{1,0:T(8,128)(2,1)}, u32[]{:S(2)}) copy-start(bf16[32,8192]{1,0:T(8,128)(2,1)} %rows_ref.1) | copy-start | bytes 1572868
  1.0 0.7 copy-start.1
  1.7 0.7 copy-start.2
  4.0 22.1 %all-to-all-start = ((bf16[8,8,8448]{2,1,0:T(8,128)(2,1)}), bf16[8,8,8448]{2,1,0:T(8,128)(2,1)S(1)}, u32[]{:S(2)}, u32[]{:S(2)}) async-start(bf16[8,8,8448]{2,1,0:T(8,128)(2,1)} %bitcast.2), calls=%async_computation | async-start | bytes 2162688 | tf_op jit(solution)/shard_map/all_to_all | solution.py:281
  10.9 15.2 %copy-start.5 = (bf16[8,8,128,128]{3,2,1,0:T(8,128)(2,1)S(1)}, bf16[8,8,128,128]{3,2,1,0:T(8,128)(2,1)}, u32[]{:S(2)}) copy-start(bf16[8,8,128,128]{3,2,1,0:T(8,128)(2,1)} %tiles_ref.2) | copy-start | bytes 6291460
  10.9 15.2 %copy-start.8 = (s32[8,8]{1,0:T(8,128)S(1)}, s32[8,8]{1,0:T(8,128)}, u32[]{:S(2)}) copy-start(s32[8,8]{1,0:T(8,128)} %where_ref.2) | copy-start | bytes 772
  26.2 20.8 %copy-start.3 = (bf16[2,8,1024,128]{3,2,1,0:T(8,128)(2,1)S(1)}, bf16[2,8,1024,128]{3,2,1,0:T(8,128)(2,1)}, u32[]{:S(2)}) copy-start(bf16[2,8,1024,128]{3,2,1,0:T(8,128)(2,1)} %keys.1) | copy-start | bytes 12582916
  26.2 20.8 %copy-start.4 = (bf16[2,8,1024,128]{3,2,1,0:T(8,128)(2,1)S(1)}, bf16[2,8,1024,128]{3,2,1,0:T(8,128)(2,1)}, u32[]{:S(2)}) copy-start(bf16[2,8,1024,128]{3,2,1,0:T(8,128)(2,1)} %values.1) | copy-start | bytes 12582916
  26.2 20.8 %copy-start.7 = (bf16[2,2,1024]{2,1,0:T(2,128)(2,1)S(1)}, bf16[2,2,1024]{2,1,0:T(2,128)(2,1)}, u32[]{:S(2)}) copy-start(bf16[2,2,1024]{2,1,0:T(2,128)(2,1)} %fresh_ref.1) | copy-start | bytes 24580
  26.2 20.8 %copy-start.10 = (s32[2]{0:T(128)S(1)}, s32[2]{0:T(128)}, u32[]{:S(2)}) copy-start(s32[2]{0:T(128)} %length_ref.1) | copy-start | bytes 28
  26.2 38.1 %slice-start = ((s8[8388608]{0:T(1024)(128)(4,1)}), s8[4194304]{0:T(1024)(128)(4,1)S(1)}, s32[]{:S(2)}) async-start(s8[8388608]{0:T(1024)(128)(4,1)} %bitcast.21), calls=%async_computation.4 | async-start | bytes 8388608
  46.9 17.4 %slice-start.1 = ((s8[8388608]{0:T(1024)(128)(4,1)}), s8[4194304]{0:T(1024)(128)(4,1)S(1)}, s32[]{:S(2)}) async-start(s8[8388608]{0:T(1024)(128)(4,1)} %bitcast.21), calls=%async_computation.5 | async-start | bytes 8388608
  47.0 17.4 %copy-start.6 = (bf16[8,8,128,128]{3,2,1,0:T(8,128)(2,1)S(1)}, bf16[8,8,128,128]{3,2,1,0:T(8,128)(2,1)}, u32[]{:S(2)}) copy-start(bf16[8,8,128,128]{3,2,1,0:T(8,128)(2,1)} %tiles_ref.3) | copy-start | bytes 6291460
  47.0 17.4 %copy-start.9 = (s32[8,8]{1,0:T(8,128)S(1)}, s32[8,8]{1,0:T(8,128)}, u32[]{:S(2)}) copy-start(s32[8,8]{1,0:T(8,128)} %where_ref.3) | copy-start | bytes 772

commit v3 on v2

--- a/solution.py
+++ b/solution.py
@@ -11,6 +11,7 @@
 BF16 = jnp.bfloat16
 I32 = jnp.int32
 LANES = 128
+CORES = 2
 EVERY = ("dp", "tensor")
 COST = pl.CostEstimate(flops=1 << 35, bytes_accessed=48 << 20, transcendentals=0)
 
@@ -27,13 +28,38 @@
     return jnp.where(mask, value, 0.0)
 
 
-def pack_kernel(per_store, tenant_ref, slot_ref, rows_ref, out_ref, place_ref):
+def pack_kernel(
+    per_store, tenant_hbm, slot_hbm, rows_hbm, out_hbm, place_ref, tenant_ref, slot_ref, rows, out, sems
+):
     group = lax.axis_index("dp")
-    count, width = rows_ref.shape
+    core = lax.axis_index("tensor") % CORES
+    count, width = rows.shape
     tenants = slot_ref.shape[1]
-    places = out_ref.shape[0]
+    places = out.shape[0]
     capacity = 8
     stores = places // capacity
+    chunks = sems.shape[1] - 2
+    step = width // chunks
+
+    def load(n):
+        source = pl.ds(pl.multiple_of(core * width + n * step, LANES), step)
+        target = pl.ds(n * step, step)
+        return pltpu.make_async_copy(rows_hbm.at[:, source], rows.at[:, target], sems.at[0, n])
+
+    def store_out(n):
+        span = pl.ds(n * step, step if n < chunks else 2 * LANES)
+        return pltpu.make_async_copy(out.at[:, span], out_hbm.at[:, span], sems.at[1, n])
+
+    small = (
+        pltpu.make_async_copy(tenant_hbm, tenant_ref, sems.at[0, chunks]),
+        pltpu.make_async_copy(slot_hbm, slot_ref, sems.at[0, chunks + 1]),
+    )
+    for copy in small:
+        copy.start()
+    for n in range(chunks):
+        load(n).start()
+    for copy in small:
+        copy.wait()
     chosen = pick(iota((tenants, count), 0) == tenant_ref[...]).astype(BF16)
     table = jnp.broadcast_to(slot_ref[...].astype(F32), (8, tenants)).astype(BF16)
     slot = dot(table, chosen)[0:1].astype(I32)
@@ -43,49 +69,72 @@
     before = dot(at_store.astype(BF16), earlier)
     rank = jnp.sum(at_store * before, axis=0, keepdims=True).astype(I32)
     placed = iota((places, count), 0) == store * capacity + rank
-    one_hot = pick(placed)
-    place_ref[...] = one_hot.astype(BF16)
-    hot = one_hot.astype(BF16)
-    step = 1024
-    for start in range(0, width, step):
-        block = dot(hot, rows_ref[:, start : start + step])
-        out_ref[:, start : start + step] = block.astype(BF16)
+    hot = pick(placed).astype(BF16)
+    place_ref[...] = hot
+    for n in range(chunks):
+        load(n).wait()
+        span = slice(n * step, (n + 1) * step)
+        out[:, span] = dot(hot, rows[:, span]).astype(BF16)
+        store_out(n).start()
     number = iota((1, count), 1) + 1
     lane_of = iota((LANES, count), 0) % (LANES // 2)
     spread = jnp.where(lane_of == group * capacity + rank, number, 0).astype(F32).astype(BF16)
     by_lane = dot(at_store.astype(BF16), spread, ((1,), (1,)))
     wide = jnp.broadcast_to(by_lane[:, None, :], (stores, capacity, LANES))
-    out_ref[:, width : width + LANES] = wide.reshape(places, LANES).astype(BF16)
+    out[:, width : width + LANES] = wide.reshape(places, LANES).astype(BF16)
     slot_col = jnp.sum(jnp.where(placed, slot + 1, 0).astype(F32), axis=1, keepdims=True)
     row_col = jnp.sum(jnp.where(placed, number, 0).astype(F32), axis=1, keepdims=True)
     lane = iota((places, LANES), 1)
     facts = jnp.where(lane == 0, slot_col, jnp.where(lane == 1, row_col, 0.0))
-    out_ref[:, width + LANES : width + 2 * LANES] = facts.astype(BF16)
+    out[:, width + LANES : width + 2 * LANES] = facts.astype(BF16)
+    store_out(chunks).start()
+    for n in range(chunks + 1):
+        store_out(n).wait()
+
+
+def in_hbm(array):
+    return pltpu.with_memory_space_constraint(array, pltpu.HBM)
 
 
 def pack_rows(row_tenant, tenant_slot, rows, places, per_store):
     count, width = rows.shape
+    half = width // CORES
+    chunks = 4
+    hbm = pl.BlockSpec(memory_space=pltpu.HBM)
     return pl.pallas_call(
         functools.partial(pack_kernel, per_store),
         out_shape=(
-            jax.ShapeDtypeStruct((places, width + 2 * LANES), BF16),
+            jax.ShapeDtypeStruct((places, half + 2 * LANES), BF16),
             jax.ShapeDtypeStruct((places, count), BF16),
         ),
-        compiler_params=pltpu.CompilerParams(vmem_limit_bytes=8 << 20),
+        in_specs=[hbm, hbm, hbm],
+        out_specs=(hbm, pl.BlockSpec(memory_space=pltpu.VMEM)),
+        scratch_shapes=[
+            pltpu.VMEM((1, count), I32),
+            pltpu.VMEM((1, tenant_slot.shape[0]), I32),
+            pltpu.VMEM((count, half), BF16),
+            pltpu.VMEM((places, half + 2 * LANES), BF16),
+            pltpu.SemaphoreType.DMA((2, chunks + 2)),
+        ],
+        compiler_params=pltpu.CompilerParams(vmem_limit_bytes=4 << 20),
         name="pack_rows",
-    )(row_tenant.reshape(1, count), tenant_slot.reshape(1, -1), rows)
-
-
-def query_kernel(where_ref, arrived_ref, tiles_ref, base_ref, out_ref, facts_ref, total):
+    )(
+        in_hbm(row_tenant.reshape(1, count)), in_hbm(tenant_slot.reshape(1, -1)), in_hbm(rows)
+    )
+
+
+def query_kernel(where_ref, mine_ref, other_ref, tiles_ref, base_ref, out_ref, facts_ref, total):
     me = lax.axis_index("dp")
+    core = lax.axis_index("tensor") % CORES
     slots, per_slot, tile = tiles_ref.shape[:3]
-    places = arrived_ref.shape[0]
-    width = arrived_ref.shape[1] - 2 * LANES
+    places = mine_ref.shape[0]
+    width = mine_ref.shape[1] - 2 * LANES
     blocks = total.shape[1] // tile
+    halves = width // tile
     group_rows = base_ref.shape[0] // blocks
     groups = out_ref.shape[0] // base_ref.shape[0]
     capacity = places // groups
-    facts = arrived_ref[:, width + LANES : width + 2 * LANES].astype(F32)
+    facts = mine_ref[:, width + LANES : width + 2 * LANES].astype(F32)
     facts_ref[...] = facts
     own_slot = facts[:, 0:1].astype(I32) - 1 - me * slots
     total[...] = jnp.zeros_like(total)
@@ -93,14 +142,16 @@
         mine = own_slot == t
         for k in range(per_slot):
             place = where_ref[t, k]
-            source = pl.multiple_of((place // blocks) * tile, tile)
-            target = pl.multiple_of((place % blocks) * tile, tile)
-            product = dot(arrived_ref[:, pl.ds(source, tile)], tiles_ref[t, k])
+            source = place // blocks
+            span = pl.ds(pl.multiple_of(source % halves * tile, tile), tile)
+            target = pl.multiple_of(place % blocks * tile, tile)
+            rows = jnp.where(source // halves == core, mine_ref[:, span], other_ref[:, span])
+            product = dot(rows, tiles_ref[t, k])
             total[:, pl.ds(target, tile)] += jnp.where(mine, product, 0.0)
     stacked = jnp.concatenate(
         [total[:, b * tile : (b + 1) * tile] for b in range(blocks)], axis=0
     ).astype(BF16)
-    by_lane = arrived_ref[:, width : width + LANES].astype(F32)
+    by_lane = mine_ref[:, width : width + LANES].astype(F32)
     by_lane = jnp.sum(by_lane.reshape(groups, capacity, LANES), axis=0)[0:1].astype(I32)
     lane = iota((1, LANES), 1)
     home = (lane % places) // capacity * group_rows + by_lane - 1
@@ -116,9 +167,9 @@
         out_ref[g * block_rows : (g + 1) * block_rows, :] = sent.astype(BF16)
 
 
-def query_visit(arrived, tiles, where, base, groups):
-    places = arrived.shape[0]
-    slots, per_slot, tile = tiles.shape[:3]
+def query_visit(mine, other, tiles, where, base, groups):
+    places = mine.shape[0]
+    tile = tiles.shape[2]
     columns = base.shape[1]
     blocks = columns // tile
     stacked = base.reshape(base.shape[0] * blocks, tile)
@@ -129,12 +180,12 @@
             jax.ShapeDtypeStruct((groups * stacked.shape[0], tile), BF16),
             jax.ShapeDtypeStruct((places, LANES), F32),
         ),
-        in_specs=[pl.BlockSpec(memory_space=pltpu.SMEM), vmem, vmem, vmem],
+        in_specs=[pl.BlockSpec(memory_space=pltpu.SMEM), vmem, vmem, vmem, vmem],
         scratch_shapes=[pltpu.VMEM((places, columns), F32)],
         cost_estimate=COST,
         compiler_params=pltpu.CompilerParams(vmem_limit_bytes=12 << 20),
         name="query_visit",
-    )(where, arrived, tiles, stacked)
+    )(where, mine, other, tiles, stacked)
 
 
 def attend_kernel(
@@ -200,9 +251,10 @@
 
 
 def output_kernel(
-    where_ref, arrived_ref, facts_ref, tiles_ref, weight, out_ref, rows, total
+    where_ref, arrived_ref, facts_ref, tiles_ref, weight, out_ref, rows_ref, total_ref
 ):
     me = lax.axis_index("dp")
+    other = 1 - lax.axis_index("tensor") % CORES
     slots, per_slot, tile = tiles_ref.shape[:3]
     groups, shards, capacity, columns = out_ref.shape
     places = groups * capacity
@@ -217,21 +269,27 @@
     lane = iota((places, arrived_ref.shape[0]), 1)
     for b in range(blocks):
         gather = pick(lane == home + b).astype(BF16)
-        rows[:, b * tile : (b + 1) * tile] = dot(gather, arrived_ref[...]).astype(BF16)
-    total[...] = jnp.zeros_like(total)
+        rows_ref[:, b * tile : (b + 1) * tile] = dot(gather, arrived_ref[...]).astype(BF16)
+    total_ref[...] = jnp.zeros_like(total_ref)
     targets = width // tile
     for t in range(slots):
         mine = own_slot == t
         for k in range(per_slot):
             place = where_ref[t, k]
-            source = pl.multiple_of((place // targets) * tile, tile)
-            target = pl.multiple_of((place % targets) * tile, tile)
-            product = dot(rows[:, pl.ds(source, tile)], tiles_ref[t, k])
-            total[:, pl.ds(target, tile)] += jnp.where(mine, product, 0.0)
+            source = pl.multiple_of(place // targets * tile, tile)
+            target = pl.multiple_of(place % targets * tile, tile)
+            product = dot(rows_ref[:, pl.ds(source, tile)], tiles_ref[t, k])
+            total_ref[:, pl.ds(target, tile)] += jnp.where(mine, product, 0.0)
+    add_base(other, rows_ref, weight, total_ref, out_ref)
+
+
+def add_base(half, rows_ref, weight, total_ref, out_ref):
+    groups, shards, capacity, columns = out_ref.shape
     for shard in range(shards):
-        span = slice(shard * columns, (shard + 1) * columns)
-        result = dot(rows[...], weight[:, span]) + total[:, span]
-        out_ref[:, shard] = result.reshape(groups, capacity, columns).astype(BF16)
+        start = (shard * CORES + half) * columns
+        span = pl.ds(pl.multiple_of(start, columns), columns)
+        result = dot(rows_ref[...], weight[:, span]) + total_ref[:, span]
+        out_ref[:, shard] = result.reshape(groups, capacity, columns).astype(out_ref.dtype)
 
 
 def output_visit(arrived, facts, tiles, where, weight, groups):
@@ -241,40 +299,60 @@
     vmem = pl.BlockSpec(memory_space=pltpu.VMEM)
     return pl.pallas_call(
         output_kernel,
-        out_shape=jax.ShapeDtypeStruct((groups, shards, places // groups, depth), BF16),
-        in_specs=[
-            pl.BlockSpec(memory_space=pltpu.SMEM),
-            vmem,
-            vmem,
-            vmem,
-            vmem,
-        ],
-        scratch_shapes=[
-            pltpu.VMEM((places, depth), BF16),
-            pltpu.VMEM((places, width), F32),
-        ],
+        out_shape=(
+            jax.ShapeDtypeStruct((groups, shards, places // groups, depth // CORES), BF16),
+            jax.ShapeDtypeStruct((places, depth), BF16),
+            jax.ShapeDtypeStruct((places, width), F32),
+        ),
+        in_specs=[pl.BlockSpec(memory_space=pltpu.SMEM), vmem, vmem, vmem, vmem],
+        out_specs=(vmem, vmem, vmem),
         cost_estimate=COST,
-        compiler_params=pltpu.CompilerParams(vmem_limit_bytes=20 << 20),
+        compiler_params=pltpu.CompilerParams(vmem_limit_bytes=16 << 20),
         name="output_visit",
     )(where, arrived, facts, tiles, weight)
 
 
+def own_kernel(rows_ref, weight, total_ref, out_ref):
+    add_base(lax.axis_index("tensor") % CORES, rows_ref, weight, total_ref, out_ref)
+
+
+def output_own(rows, weight, total, shape):
+    vmem = pl.BlockSpec(memory_space=pltpu.VMEM)
+    return pl.pallas_call(
+        own_kernel,
+        out_shape=jax.ShapeDtypeStruct(shape, F32),
+        in_specs=[vmem, vmem, vmem],
+        out_specs=vmem,
+        cost_estimate=COST,
+        compiler_params=pltpu.CompilerParams(vmem_limit_bytes=16 << 20),
+        name="output_own",
+    )(rows, weight, total)
+
+
 def finish_kernel(arrived_ref, place_ref, out_ref):
-    stores, shards, capacity, columns = arrived_ref.shape
-    total = arrived_ref[:, 0].astype(F32)
-    for j in range(1, shards):
-        total = total + arrived_ref[:, j].astype(F32)
-    rounded = total.reshape(stores * capacity, columns).astype(BF16)
-    out_ref[...] = dot(place_ref[...], rounded, ((0,), (0,))).astype(BF16)
+    stores, pairs, cores, capacity, columns = arrived_ref.shape
+    for core in range(cores):
+        total = arrived_ref[:, 0, core].astype(F32)
+        for pair in range(1, pairs):
+            total = total + arrived_ref[:, pair, core].astype(F32)
+        rounded = total.reshape(stores * capacity, columns).astype(BF16)
+        span = slice(core * columns, (core + 1) * columns)
+        out_ref[:, span] = dot(place_ref[...], rounded, ((0,), (0,))).astype(BF16)
 
 
 def finish(arrived, place):
+    cores, columns = arrived.shape[2], arrived.shape[4]
     return pl.pallas_call(
         finish_kernel,
-        out_shape=jax.ShapeDtypeStruct((place.shape[1], arrived.shape[3]), BF16),
+        out_shape=jax.ShapeDtypeStruct((place.shape[1], cores * columns), BF16),
         compiler_params=pltpu.CompilerParams(vmem_limit_bytes=8 << 20),
         name="finish",
     )(arrived, place)
+
+
+def across_chip(block):
+    count = lax.axis_size("tensor")
+    return lax.ppermute(block, "tensor", [(i, i ^ 1) for i in range(count)])
 
 
 def swap(blocks, axes):
@@ -301,17 +379,26 @@
     per_store = query_deltas.shape[0]
     capacity = 8
     packed, place = pack_rows(row_tenant, tenant_slot, activations, groups * capacity, per_store)
-    arrived = swap(packed, "dp")
+    arrived = swap(packed.reshape(groups, capacity, -1), "dp").reshape(packed.shape)
     base_query = jnp.dot(activations, query_weight, preferred_element_type=F32)
-    sent_query, facts = query_visit(arrived, query_deltas, query_where, base_query, groups)
+    arrived, base_query = lax.optimization_barrier((arrived, base_query))
+    other = across_chip(arrived)
+    sent_query, facts = query_visit(
+        arrived, other, query_deltas, query_where, base_query, groups
+    )
     query = swap(sent_query, EVERY)
     attended = attend(query, key_cache, value_cache, fresh_pair, cache_length, groups)
     size = attended.shape[3]
     rows = swap(attended.reshape(-1, size), EVERY)
-    parts = output_visit(rows, facts, output_deltas, output_where, output_weight, groups)
+    sent, visitors, delta = output_visit(
+        rows, facts, output_deltas, output_where, output_weight, groups
+    )
+    received = across_chip(sent)
+    own = output_own(visitors, output_weight, delta, sent.shape)
+    parts = (own + received.astype(F32)).astype(BF16)
     columns = parts.shape[3]
     summed = swap(parts.reshape(-1, columns), EVERY)
-    return finish(summed.reshape(groups, shards, capacity, columns), place)
+    return finish(summed.reshape(groups, shards // CORES, CORES, capacity, columns), place)
 
 
 def solution(mesh):

time: 91.6 us -> 82.7 us (0.903)
  blocking collectives: 57 us -> 49.5 us
  waiting for transfers between devices: 9.99 us -> 6.5 us
  starting transfers between devices: 6.86 us -> 9.79 us
  local copies, waits for them, and re-layouts: 2.42 us -> 0.06 us
  Pallas kernels: 9.74 us -> 11.1 us
    all_to_all x3, blocking collectives: 57 us -> 49.5 us  [swap(): return lax.all_to_all(blocks, axes, split_axis=0, concat_axis=0, tiled=True)]
    all_to_all x1, waiting for transfers between devices: 9.99 us -> 4.36 us  [swap(): return lax.all_to_all(blocks, axes, split_axis=0, concat_axis=0, tiled=True)]
    ppermute x0 -> x2, starting transfers between devices: none -> 2.93 us  [across_chip(): return lax.ppermute(block, 'tensor', [(i, i ^ 1) for i in range(count)])]
    unnamed x26 -> x20, local copies, waits for them, and re-layouts: 2.4 us -> 0.05 us
    ppermute x0 -> x2, waiting for transfers between devices: none -> 2.14 us  [across_chip(): return lax.ppermute(block, 'tensor', [(i, i ^ 1) for i in range(count)])]
    pallas_call x1 -> x2, Pallas kernels: 3.15 us -> 3.51 us  [the longest x1 2.58 us: output_visit(): pl.pallas_call(output_kernel, out_shape=(jax.ShapeDtypeStruct((groups, sh...]
  transfers between devices with their start and end apart: 1 -> 3, of which waited for: 1 -> 3; matrix products, arithmetic and copies ran while one was open for 6% -> 6% of each run, Pallas kernels for 0% -> 1%
where the time goes in v3:
time: 82.7 us; the launch traced here: 82.4 us
  blocking collectives  49.5 us (60%)
  Pallas kernels  11.1 us (13%)
  starting transfers between devices  9.79 us (12%)
  waiting for transfers between devices  6.5 us (8%)
  matrix products  5.2 us (6%)
    all_to_all x3, blocking collectives, swap(): return lax.all_to_all(blocks, axes, split_axis=0, concat_axis=0, tiled=True)  49.5 us
    all_to_all x1, starting transfers between devices, swap(): return lax.all_to_all(blocks, axes, split_axis=0, concat_axis=0, tiled=True)  6.87 us
    dot_general x1, matrix products, body(): base_query = jnp.dot(activations, query_weight, preferred_element_type=F32)  5.2 us
    all_to_all x1, waiting for transfers between devices, swap(): return lax.all_to_all(blocks, axes, split_axis=0, concat_axis=0, tiled=True)  4.36 us
    ppermute x2, starting transfers between devices, across_chip(): return lax.ppermute(block, 'tensor', [(i, i ^ 1) for i in range(count)])  2.93 us
    pallas_call x1, Pallas kernels, output_visit(): pl.pallas_call(output_kernel, out_shape=(jax.ShapeDtypeStruct((groups, sh...  2.58 us
    pallas_call x1, Pallas kernels, attend(): pl.pallas_call(attend_kernel, out_shape=jax.ShapeDtypeStruct((groups, sha...  2.37 us
    pallas_call x1, Pallas kernels, pack_rows(): pl.pallas_call(functools.partial(pack_kernel, per_store), out_shape=(jax....  2.37 us
  transfers between devices with their start and end apart: 3, of which 3 were waited for; matrix products, arithmetic and copies ran while one was open for 6% of the time, Pallas kernels for 1%

profile of v3, /device:TPU:1, one launch (start us, length us, event | category | flops | bytes accessed | tf_op | source)
XLA Modules:
  0.0 82.4 jit_solution(15705264769683582537)
XLA Ops:
  0.0 2.4 %pack_rows.1 = (bf16[64,4352]{1,0:T(8,128)(2,1)}, bf16[64,32]{1,0:T(8,128)(2,1)S(1)}) custom-call(s32[1,32]{1,0:T(1,128)} %bitcast.22, s32[1,64]{1,0:T(1,128)} %bitcast.23, bf16[32,8192]{1,0:T(8,128)(2,1)} %rows_hbm.1), custom_call_target="tpu_custom_call" | custom-call | tf_op jit(solution)/shard_map/pack_rows/pallas_call | solution.py:104
  2.4 6.9 %all-to-all-start = ((bf16[8,8,4352]{2,1,0:T(8,128)(2,1)}), bf16[8,8,4352]{2,1,0:T(8,128)(2,1)S(1)}, u32[]{:S(2)}, u32[]{:S(2)}) async-start(bf16[8,8,4352]{2,1,0:T(8,128)(2,1)} %bitcast.2), calls=%async_computation | async-start | bytes 1114112 | tf_op jit(solution)/shard_map/all_to_all | solution.py:359
  9.2 0.0 copy-start.2
  9.2 0.0 copy-start.5
  9.3 5.2 %fusion = f32[32,512]{1,0:T(8,128)S(1)} fusion(bf16[32,8192]{1,0:T(8,128)(2,1)} %rows_hbm.1, bf16[8192,512]{1,0:T(8,128)(2,1)} %param.14), kind=kOutput, calls=%fused_computation.1 | convolution fusion | flops 268435456 | bytes 8978432 | tf_op jit(solution)/shard_map/dot_general | solution.py:383
  14.5 4.4 %all-to-all-done = bf16[8,8,4352]{2,1,0:T(8,128)(2,1)S(1)} async-done(((bf16[8,8,4352]{2,1,0:T(8,128)(2,1)}), bf16[8,8,4352]{2,1,0:T(8,128)(2,1)S(1)}, u32[]{:S(2)}, u32[]{:S(2)}) %all-to-all-start) | async-done | bytes 557088 | tf_op jit(solution)/shard_map/all_to_all | solution.py:359
  18.8 1.8 %collective-permute-start = (bf16[64,4352]{1,0:T(8,128)(2,1)S(1)}, bf16[64,4352]{1,0:T(8,128)(2,1)S(1)}, u32[]{:S(2)}, u32[]{:S(2)}) collective-permute-start(bf16[64,4352]{1,0:T(8,128)(2,1)S(1)} %bitcast.13), channel_id=1, source_target_pairs={{0,1},{1,0},{2,3},{3,2},{4,5},{5,4},{6,7},{7,6},{8,9},{9,8},{10,11... | collective-permute-start | bytes 1671176 | tf_op jit(solution)/shard_map/ppermute | solution.py:355
  20.6 0.0 copy-start
  20.6 0.0 copy-start.1
  20.6 0.0 copy-start.4
  20.7 0.0 copy-start.7
  20.7 1.5 %collective-permute-done.other_ref = bf16[64,4352]{1,0:T(8,128)(2,1)S(1)} collective-permute-done((bf16[64,4352]{1,0:T(8,128)(2,1)S(1)}, bf16[64,4352]{1,0:T(8,128)(2,1)S(1)}, u32[]{:S(2)}, u32[]{:S(2)}) %collective-permute-start) | collective-permute-done | bytes 557088 | tf_op jit(solution)/shard_map/ppermute | solution.py:355
  22.2 0.0 copy-done.2
  22.2 0.0 copy-done.5
  22.2 0.0 slice-start
  22.2 2.1 %query_visit.1 = (bf16[1024,128]{1,0:T(8,128)(2,1)S(1)}, f32[64,128]{1,0:T(8,128)S(1)}) custom-call(s32[8,8]{1,0:T(8,128)S(1)} %copy-done.5, bf16[64,4352]{1,0:T(8,128)(2,1)S(1)} %bitcast.14, bf16[64,4352]{1,0:T(8,128)(2,1)S(1)} %collective-permute-done.other_ref, bf16[8,8,128,128]{3,2,1,0:T(8,128)(2,1)S(1)} %copy-done.2, f32[128,128]{1,0:T(8,128)S(1)} %reshape.37.base_ref), custom_call_target="tpu_custom_call" | custom-call | flops 34359738368 | bytes 50331648 | tf_op jit(solution)/shard_map/query_visit/pallas_call | solution.py:177
  24.3 17.6 %all_to_all.34 = bf16[128,8,128]{2,1,0:T(8,128)(2,1)S(1)} all-to-all(bf16[128,8,128]{2,1,0:T(8,128)(2,1)S(1)} %bitcast.16), channel_id=1, replica_groups=mesh['dp'=8,'tensor'=16] {'dp','tensor'}, dimensions={0} | all-to-all | bytes 524288 | tf_op jit(solution)/shard_map/all_to_all | solution.py:359
  41.9 0.0 slice-start.1
  41.9 0.0 copy-done
  41.9 0.0 copy-done.1
  41.9 0.0 copy-done.4
  41.9 0.0 copy-done.7
  41.9 0.0 copy-start.3
  41.9 0.0 copy-start.6
  42.0 2.4 %attend.1 = bf16[8,16,8,128]{3,2,1,0:T(8,128)(2,1)S(1)} custom-call(s32[2]{0:T(128)S(1)} %copy-done.7, bf16[8,16,8,128]{3,2,1,0:T(8,128)(2,1)S(1)} %bitcast.17, bf16[2,2,1024]{2,1,0:T(2,128)(2,1)S(1)} %copy-done.4, bf16[2,8,1024,128]{3,2,1,0:T(8,128)(2,1)S(1)} %copy-done, bf16[2,8,1024,128]{3,2,1,0:T(8,128)(2,1)S(1)} %copy-done.1), custom_call_target="tpu_custom_call" | custom-call | flops 34359738368 | bytes 50331648 | tf_op jit(solution)/shard_map/attend/pallas_call | solution.py:243
  44.3 15.0 %all_to_all.35 = bf16[128,8,128]{2,1,0:T(8,128)(2,1)S(1)} all-to-all(bf16[128,8,128]{2,1,0:T(8,128)(2,1)S(1)} %bitcast.18), channel_id=1, replica_groups=mesh['dp'=8,'tensor'=16] {'dp','tensor'}, dimensions={0} | all-to-all | bytes 524288 | tf_op jit(solution)/shard_map/all_to_all | solution.py:359
  59.3 0.0 slice-done
  59.3 0.0 slice-done.1
  59.3 0.0 copy-done.3
  59.3 0.0 copy-done.6
  59.3 2.6 %output_visit.1 = (bf16[8,16,8,256]{3,2,1,0:T(8,128)(2,1)S(1)}, bf16[64,512]{1,0:T(8,128)(2,1)S(1)}, f32[64,8192]{1,0:T(8,128)S(1)}) custom-call(s32[8,8]{1,0:T(8,128)S(1)} %copy-done.6, bf16[1024,128]{1,0:T(8,128)(2,1)S(1)} %bitcast.15, f32[64,128]{1,0:T(8,128)S(1)} %get-tuple-element.18.facts_ref, bf16[8,8,128,128]{3,2,1,0:T(8,128)(2,1)S(1)} %copy-done.3, ...), custom_call_target="tpu_custom_call" | custom-call | flops 34359738368 | bytes 50331648 | tf_op jit(solution)/shard_map/output_visit/pallas_call | solution.py:300
  61.9 1.1 %collective-permute-start.1 = (bf16[8,16,8,256]{3,2,1,0:T(8,128)(2,1)S(1)}, bf16[8,16,8,256]{3,2,1,0:T(8,128)(2,1)S(1)}, u32[]{:S(2)}, u32[]{:S(2)}) collective-permute-start(bf16[8,16,8,256]{3,2,1,0:T(8,128)(2,1)S(1)} %get-tuple-element.21), channel_id=1, source_target_pairs={{0,1},{1,0},{2,3},{3,2},{4,5},{5,4},{6,7},{7,6},{8,9},{9,8},{10,11... | collective-permute-start | bytes 1572872 | tf_op jit(solution)/shard_map/ppermute | solution.py:355
  63.0 0.9 %output_own.1 = f32[8,16,8,256]{3,2,1,0:T(8,128)S(1)} custom-call(bf16[64,512]{1,0:T(8,128)(2,1)S(1)} %get-tuple-element.19.rows_ref, bf16[512,8192]{1,0:T(8,128)(2,1)S(1)} %bitcast.20, f32[64,8192]{1,0:T(8,128)S(1)} %get-tuple-element.20.total_ref), custom_call_target="tpu_custom_call" | custom-call | flops 34359738368 | bytes 50331648 | tf_op jit(solution)/shard_map/output_own/pallas_call | solution.py:321
  64.0 0.6 collective-permute-done.1
  64.6 0.1 add_convert_fusion
  64.7 17.0 %all_to_all.36 = bf16[128,8,256]{2,1,0:T(8,128)(2,1)S(1)} all-to-all(bf16[128,8,256]{2,1,0:T(8,128)(2,1)S(1)} %bitcast.21), channel_id=1, replica_groups=mesh['dp'=8,'tensor'=16] {'dp','tensor'}, dimensions={0} | all-to-all | bytes 1048576 | tf_op jit(solution)/shard_map/all_to_all | solution.py:359
  81.6 0.8 finish.1
  (2 shorter events, 0.0 us)
Async XLA Ops:
  2.4 16.4 %all-to-all-start = ((bf16[8,8,4352]{2,1,0:T(8,128)(2,1)}), bf16[8,8,4352]{2,1,0:T(8,128)(2,1)S(1)}, u32[]{:S(2)}, u32[]{:S(2)}) async-start(bf16[8,8,4352]{2,1,0:T(8,128)(2,1)} %bitcast.2), calls=%async_computation | async-start | bytes 1114112 | tf_op jit(solution)/shard_map/all_to_all | solution.py:359
  9.2 13.0 %copy-start.2 = (bf16[8,8,128,128]{3,2,1,0:T(8,128)(2,1)S(1)}, bf16[8,8,128,128]{3,2,1,0:T(8,128)(2,1)}, u32[]{:S(2)}) copy-start(bf16[8,8,128,128]{3,2,1,0:T(8,128)(2,1)} %tiles_ref.2) | copy-start | bytes 6291460
  9.2 13.0 %copy-start.5 = (s32[8,8]{1,0:T(8,128)S(1)}, s32[8,8]{1,0:T(8,128)}, u32[]{:S(2)}) copy-start(s32[8,8]{1,0:T(8,128)} %where_ref.2) | copy-start | bytes 772
  18.8 3.4 %collective-permute-start = (bf16[64,4352]{1,0:T(8,128)(2,1)S(1)}, bf16[64,4352]{1,0:T(8,128)(2,1)S(1)}, u32[]{:S(2)}, u32[]{:S(2)}) collective-permute-start(bf16[64,4352]{1,0:T(8,128)(2,1)S(1)} %bitcast.13), channel_id=1, source_target_pairs={{0,1},{1,0},{2,3},{3,2},{4,5},{5,4},{6,7},{7,6},{8,9},{9,8},{10,11... | collective-permute-start | bytes 1671176 | tf_op jit(solution)/shard_map/ppermute | solution.py:355
  20.6 21.3 %copy-start = (bf16[2,8,1024,128]{3,2,1,0:T(8,128)(2,1)S(1)}, bf16[2,8,1024,128]{3,2,1,0:T(8,128)(2,1)}, u32[]{:S(2)}) copy-start(bf16[2,8,1024,128]{3,2,1,0:T(8,128)(2,1)} %keys.1) | copy-start | bytes 12582916
  20.6 21.3 %copy-start.1 = (bf16[2,8,1024,128]{3,2,1,0:T(8,128)(2,1)S(1)}, bf16[2,8,1024,128]{3,2,1,0:T(8,128)(2,1)}, u32[]{:S(2)}) copy-start(bf16[2,8,1024,128]{3,2,1,0:T(8,128)(2,1)} %values.1) | copy-start | bytes 12582916
  20.6 21.3 %copy-start.4 = (bf16[2,2,1024]{2,1,0:T(2,128)(2,1)S(1)}, bf16[2,2,1024]{2,1,0:T(2,128)(2,1)}, u32[]{:S(2)}) copy-start(bf16[2,2,1024]{2,1,0:T(2,128)(2,1)} %fresh_ref.1) | copy-start | bytes 24580
  20.7 21.3 %copy-start.7 = (s32[2]{0:T(128)S(1)}, s32[2]{0:T(128)}, u32[]{:S(2)}) copy-start(s32[2]{0:T(128)} %length_ref.1) | copy-start | bytes 28
  22.2 37.1 %slice-start = ((s8[8388608]{0:T(1024)(128)(4,1)}), s8[4194304]{0:T(1024)(128)(4,1)S(1)}, s32[]{:S(2)}) async-start(s8[8388608]{0:T(1024)(128)(4,1)} %bitcast.19), calls=%async_computation.4 | async-start | bytes 8388608
  41.9 17.4 %slice-start.1 = ((s8[8388608]{0:T(1024)(128)(4,1)}), s8[4194304]{0:T(1024)(128)(4,1)S(1)}, s32[]{:S(2)}) async-start(s8[8388608]{0:T(1024)(128)(4,1)} %bitcast.19), calls=%async_computation.5 | async-start | bytes 8388608
  41.9 17.4 %copy-start.3 = (bf16[8,8,128,128]{3,2,1,0:T(8,128)(2,1)S(1)}, bf16[8,8,128,128]{3,2,1,0:T(8,128)(2,1)}, u32[]{:S(2)}) copy-start(bf16[8,8,128,128]{3,2,1,0:T(8,128)(2,1)} %tiles_ref.3) | copy-start | bytes 6291460
  41.9 17.4 %copy-start.6 = (s32[8,8]{1,0:T(8,128)S(1)}, s32[8,8]{1,0:T(8,128)}, u32[]{:S(2)}) copy-start(s32[8,8]{1,0:T(8,128)} %where_ref.3) | copy-start | bytes 772
  61.9 2.7 %collective-permute-start.1 = (bf16[8,16,8,256]{3,2,1,0:T(8,128)(2,1)S(1)}, bf16[8,16,8,256]{3,2,1,0:T(8,128)(2,1)S(1)}, u32[]{:S(2)}, u32[]{:S(2)}) collective-permute-start(bf16[8,16,8,256]{3,2,1,0:T(8,128)(2,1)S(1)} %get-tuple-element.21), channel_id=1, source_target_pairs={{0,1},{1,0},{2,3},{3,2},{4,5},{5,4},{6,7},{7,6},{8,9},{9,8},{10,11... | collective-permute-start | bytes 1572872 | tf_op jit(solution)/shard_map/ppermute | solution.py:355

commit v4 on v3

--- a/solution.py
+++ b/solution.py
@@ -24,12 +24,16 @@
     return lax.dot_general(a, b, (contract, ((), ())), preferred_element_type=F32)
 
 
+def log2(size):
+    return size.bit_length() - 1
+
+
 def pick(mask, value=1.0):
     return jnp.where(mask, value, 0.0)
 
 
 def pack_kernel(
-    per_store, tenant_hbm, slot_hbm, rows_hbm, out_hbm, place_ref, tenant_ref, slot_ref, rows, out, sems
+    per_store, tenant_hbm, slot_hbm, rows_hbm, out, place_ref, tenant_ref, slot_ref, rows, sems
 ):
     group = lax.axis_index("dp")
     core = lax.axis_index("tensor") % CORES
@@ -38,21 +42,17 @@
     places = out.shape[0]
     capacity = 8
     stores = places // capacity
-    chunks = sems.shape[1] - 2
+    chunks = sems.shape[0] - 2
     step = width // chunks
 
     def load(n):
         source = pl.ds(pl.multiple_of(core * width + n * step, LANES), step)
         target = pl.ds(n * step, step)
-        return pltpu.make_async_copy(rows_hbm.at[:, source], rows.at[:, target], sems.at[0, n])
-
-    def store_out(n):
-        span = pl.ds(n * step, step if n < chunks else 2 * LANES)
-        return pltpu.make_async_copy(out.at[:, span], out_hbm.at[:, span], sems.at[1, n])
+        return pltpu.make_async_copy(rows_hbm.at[:, source], rows.at[:, target], sems.at[n])
 
     small = (
-        pltpu.make_async_copy(tenant_hbm, tenant_ref, sems.at[0, chunks]),
-        pltpu.make_async_copy(slot_hbm, slot_ref, sems.at[0, chunks + 1]),
+        pltpu.make_async_copy(tenant_hbm, tenant_ref, sems.at[chunks]),
+        pltpu.make_async_copy(slot_hbm, slot_ref, sems.at[chunks + 1]),
     )
     for copy in small:
         copy.start()
@@ -75,7 +75,6 @@
         load(n).wait()
         span = slice(n * step, (n + 1) * step)
         out[:, span] = dot(hot, rows[:, span]).astype(BF16)
-        store_out(n).start()
     number = iota((1, count), 1) + 1
     lane_of = iota((LANES, count), 0) % (LANES // 2)
     spread = jnp.where(lane_of == group * capacity + rank, number, 0).astype(F32).astype(BF16)
@@ -87,9 +86,6 @@
     lane = iota((places, LANES), 1)
     facts = jnp.where(lane == 0, slot_col, jnp.where(lane == 1, row_col, 0.0))
     out[:, width + LANES : width + 2 * LANES] = facts.astype(BF16)
-    store_out(chunks).start()
-    for n in range(chunks + 1):
-        store_out(n).wait()
 
 
 def in_hbm(array):
@@ -101,6 +97,7 @@
     half = width // CORES
     chunks = 4
     hbm = pl.BlockSpec(memory_space=pltpu.HBM)
+    vmem = pl.BlockSpec(memory_space=pltpu.VMEM)
     return pl.pallas_call(
         functools.partial(pack_kernel, per_store),
         out_shape=(
@@ -108,14 +105,14 @@
             jax.ShapeDtypeStruct((places, count), BF16),
         ),
         in_specs=[hbm, hbm, hbm],
-        out_specs=(hbm, pl.BlockSpec(memory_space=pltpu.VMEM)),
+        out_specs=(vmem, vmem),
         scratch_shapes=[
             pltpu.VMEM((1, count), I32),
             pltpu.VMEM((1, tenant_slot.shape[0]), I32),
             pltpu.VMEM((count, half), BF16),
-            pltpu.VMEM((places, half + 2 * LANES), BF16),
-            pltpu.SemaphoreType.DMA((2, chunks + 2)),
+            pltpu.SemaphoreType.DMA((chunks + 2,)),
         ],
+        cost_estimate=COST,
         compiler_params=pltpu.CompilerParams(vmem_limit_bytes=4 << 20),
         name="pack_rows",
     )(
@@ -123,34 +120,23 @@
     )
 
 
-def query_kernel(where_ref, mine_ref, other_ref, tiles_ref, base_ref, out_ref, facts_ref, total):
+def query_kernel(
+    group_rows, where_vmem, mine_ref, other_ref, tiles_ref, base_ref, out_ref, facts_ref, where_ref, sem, expand, *totals
+):
+    fetch = pltpu.make_async_copy(where_vmem, where_ref, sem)
+    fetch.start()
     me = lax.axis_index("dp")
     core = lax.axis_index("tensor") % CORES
     slots, per_slot, tile = tiles_ref.shape[:3]
     places = mine_ref.shape[0]
     width = mine_ref.shape[1] - 2 * LANES
-    blocks = total.shape[1] // tile
     halves = width // tile
-    group_rows = base_ref.shape[0] // blocks
-    groups = out_ref.shape[0] // base_ref.shape[0]
+    groups = lax.axis_size("dp")
+    blocks = base_ref.shape[0] // group_rows
     capacity = places // groups
     facts = mine_ref[:, width + LANES : width + 2 * LANES].astype(F32)
     facts_ref[...] = facts
     own_slot = facts[:, 0:1].astype(I32) - 1 - me * slots
-    total[...] = jnp.zeros_like(total)
-    for t in range(slots):
-        mine = own_slot == t
-        for k in range(per_slot):
-            place = where_ref[t, k]
-            source = place // blocks
-            span = pl.ds(pl.multiple_of(source % halves * tile, tile), tile)
-            target = pl.multiple_of(place % blocks * tile, tile)
-            rows = jnp.where(source // halves == core, mine_ref[:, span], other_ref[:, span])
-            product = dot(rows, tiles_ref[t, k])
-            total[:, pl.ds(target, tile)] += jnp.where(mine, product, 0.0)
-    stacked = jnp.concatenate(
-        [total[:, b * tile : (b + 1) * tile] for b in range(blocks)], axis=0
-    ).astype(BF16)
     by_lane = mine_ref[:, width : width + LANES].astype(F32)
     by_lane = jnp.sum(by_lane.reshape(groups, capacity, LANES), axis=0)[0:1].astype(I32)
     lane = iota((1, LANES), 1)
@@ -159,12 +145,34 @@
     block_rows = group_rows * blocks
     for g in range(groups):
         row = iota((block_rows, LANES), 0) + g * block_rows
-        expand = jnp.concatenate(
-            [pick(row == home + b).astype(BF16) for b in range(0, blocks, LANES // places)],
-            axis=1,
-        )
-        sent = dot(expand, stacked) + jnp.where(me == g, base_ref[...], 0.0)
-        out_ref[g * block_rows : (g + 1) * block_rows, :] = sent.astype(BF16)
+        for n, b in enumerate(range(0, blocks, LANES // places)):
+            one_hot = pick(row == home + b).astype(BF16)
+            expand[g * block_rows : (g + 1) * block_rows, n * LANES : (n + 1) * LANES] = one_hot
+    for total in totals:
+        total[...] = jnp.zeros_like(total)
+    fetch.wait()
+    for t in range(slots):
+        mine = own_slot == t
+        for k in range(per_slot):
+            place = where_ref[t, k]
+            source = lax.shift_right_logical(place, log2(blocks))
+            start = lax.shift_left(source & (halves - 1), log2(tile))
+            target = lax.shift_left(place & (blocks - 1), log2(tile))
+            span = pl.ds(pl.multiple_of(start, tile), tile)
+            own_half = lax.shift_right_logical(source, log2(halves)) == core
+            rows = jnp.where(own_half, mine_ref[:, span], other_ref[:, span])
+            product = dot(rows, tiles_ref[t, k])
+            total = totals[k % len(totals)]
+            total[:, pl.ds(pl.multiple_of(target, tile), tile)] += jnp.where(mine, product, 0.0)
+    whole = totals[0][...]
+    for total in totals[1:]:
+        whole = whole + total[...]
+    sums = [whole[:, b * tile : (b + 1) * tile] for b in range(blocks)]
+    stacked = jnp.concatenate(sums, axis=0).astype(BF16)
+    for g in range(groups):
+        span = slice(g * block_rows, (g + 1) * block_rows)
+        sent = dot(expand[span, :], stacked) + jnp.where(me == g, base_ref[...], 0.0)
+        out_ref[span, :] = sent.astype(BF16)
 
 
 def query_visit(mine, other, tiles, where, base, groups):
@@ -175,13 +183,18 @@
     stacked = base.reshape(base.shape[0] * blocks, tile)
     vmem = pl.BlockSpec(memory_space=pltpu.VMEM)
     return pl.pallas_call(
-        query_kernel,
+        functools.partial(query_kernel, base.shape[0]),
         out_shape=(
             jax.ShapeDtypeStruct((groups * stacked.shape[0], tile), BF16),
             jax.ShapeDtypeStruct((places, LANES), F32),
         ),
-        in_specs=[pl.BlockSpec(memory_space=pltpu.SMEM), vmem, vmem, vmem, vmem],
-        scratch_shapes=[pltpu.VMEM((places, columns), F32)],
+        in_specs=[vmem] * 5,
+        scratch_shapes=[
+            pltpu.SMEM(where.shape, I32),
+            pltpu.SemaphoreType.DMA,
+            pltpu.VMEM((groups * stacked.shape[0], places * blocks), BF16),
+        ]
+        + [pltpu.VMEM((places, columns), F32)] * 4,
         cost_estimate=COST,
         compiler_params=pltpu.CompilerParams(vmem_limit_bytes=12 << 20),
         name="query_visit",
@@ -189,8 +202,10 @@
 
 
 def attend_kernel(
-    length_ref, arrived_ref, fresh_ref, keys, values, out_ref
+    length_vmem, arrived_ref, fresh_ref, keys, values, out_ref, length_ref, sem
 ):
+    fetch = pltpu.make_async_copy(length_vmem, length_ref, sem)
+    fetch.start()
     requests, kv_heads, context, size = keys.shape
     shards = out_ref.shape[1]
     stores = arrived_ref.shape[0]
@@ -201,6 +216,7 @@
     fresh = fresh_ref[...].astype(F32)
     upper = iota((8, size), 0) < 4
     position = iota((1, context), 1)
+    fetch.wait()
     mixed = [[None] * kv_heads for _ in range(requests)]
     for i in range(requests):
         visible = position < length_ref[i]
@@ -243,7 +259,8 @@
     return pl.pallas_call(
         attend_kernel,
         out_shape=jax.ShapeDtypeStruct((groups, shards, 8, size), BF16),
-        in_specs=[pl.BlockSpec(memory_space=pltpu.SMEM), vmem, vmem, vmem, vmem],
+        in_specs=[vmem] * 5,
+        scratch_shapes=[pltpu.SMEM(lengths.shape, I32), pltpu.SemaphoreType.DMA],
         cost_estimate=COST,
         compiler_params=pltpu.CompilerParams(vmem_limit_bytes=16 << 20),
         name="attend",
@@ -251,8 +268,10 @@
 
 
 def output_kernel(
-    where_ref, arrived_ref, facts_ref, tiles_ref, weight, out_ref, rows_ref, total_ref
+    where_vmem, arrived_ref, facts_ref, tiles_ref, weight, out_ref, rows_ref, total_ref, where_ref, sem, hold
 ):
+    fetch = pltpu.make_async_copy(where_vmem, where_ref, sem)
+    fetch.start()
     me = lax.axis_index("dp")
     other = 1 - lax.axis_index("tensor") % CORES
     slots, per_slot, tile = tiles_ref.shape[:3]
@@ -266,30 +285,33 @@
     number = facts[:, 1:2]
     home = iota((places, 1), 0) // capacity * group_rows + number - 1
     home = jnp.where(number > 0, home * blocks, -blocks)
+    total_ref[...] = jnp.zeros_like(total_ref)
     lane = iota((places, arrived_ref.shape[0]), 1)
+    gather = jnp.concatenate([pick(lane == home + b).astype(BF16) for b in range(blocks)], axis=0)
+    gathered = dot(gather, arrived_ref[...]).astype(BF16)
     for b in range(blocks):
-        gather = pick(lane == home + b).astype(BF16)
-        rows_ref[:, b * tile : (b + 1) * tile] = dot(gather, arrived_ref[...]).astype(BF16)
-    total_ref[...] = jnp.zeros_like(total_ref)
+        rows_ref[:, b * tile : (b + 1) * tile] = gathered[b * places : (b + 1) * places]
     targets = width // tile
-    for t in range(slots):
-        mine = own_slot == t
-        for k in range(per_slot):
+    fetch.wait()
+    every = slots * per_slot // shards
+    for shard in range(shards):
+        for n in range(shard * every, (shard + 1) * every):
+            t, k = n // per_slot, n % per_slot
             place = where_ref[t, k]
-            source = pl.multiple_of(place // targets * tile, tile)
-            target = pl.multiple_of(place % targets * tile, tile)
-            product = dot(rows_ref[:, pl.ds(source, tile)], tiles_ref[t, k])
-            total_ref[:, pl.ds(target, tile)] += jnp.where(mine, product, 0.0)
-    add_base(other, rows_ref, weight, total_ref, out_ref)
-
-
-def add_base(half, rows_ref, weight, total_ref, out_ref):
-    groups, shards, capacity, columns = out_ref.shape
+            source = lax.shift_left(lax.shift_right_logical(place, log2(targets)), log2(tile))
+            target = lax.shift_left(place & (targets - 1), log2(tile))
+            rows = rows_ref[:, pl.ds(pl.multiple_of(source, tile), tile)]
+            product = dot(rows, tiles_ref[t, k])
+            span = pl.ds(pl.multiple_of(target, tile), tile)
+            total_ref[:, span] += jnp.where(own_slot == t, product, 0.0)
+        hold[shard] = dot(rows_ref[...], weight[:, columns_of(shard, other, columns)])
     for shard in range(shards):
-        start = (shard * CORES + half) * columns
-        span = pl.ds(pl.multiple_of(start, columns), columns)
-        result = dot(rows_ref[...], weight[:, span]) + total_ref[:, span]
-        out_ref[:, shard] = result.reshape(groups, capacity, columns).astype(out_ref.dtype)
+        result = hold[shard] + total_ref[:, columns_of(shard, other, columns)]
+        out_ref[:, shard] = result.reshape(groups, capacity, columns).astype(BF16)
+
+
+def columns_of(shard, half, columns):
+    return pl.ds(pl.multiple_of((shard * CORES + half) * columns, columns), columns)
 
 
 def output_visit(arrived, facts, tiles, where, weight, groups):
@@ -304,8 +326,9 @@
             jax.ShapeDtypeStruct((places, depth), BF16),
             jax.ShapeDtypeStruct((places, width), F32),
         ),
-        in_specs=[pl.BlockSpec(memory_space=pltpu.SMEM), vmem, vmem, vmem, vmem],
+        in_specs=[vmem] * 5,
         out_specs=(vmem, vmem, vmem),
+        scratch_shapes=[pltpu.SMEM(where.shape, I32), pltpu.SemaphoreType.DMA, pltpu.VMEM((shards, places, depth // CORES), F32)],
         cost_estimate=COST,
         compiler_params=pltpu.CompilerParams(vmem_limit_bytes=16 << 20),
         name="output_visit",
@@ -313,7 +336,12 @@
 
 
 def own_kernel(rows_ref, weight, total_ref, out_ref):
-    add_base(lax.axis_index("tensor") % CORES, rows_ref, weight, total_ref, out_ref)
+    core = lax.axis_index("tensor") % CORES
+    groups, shards, capacity, columns = out_ref.shape
+    for shard in range(shards):
+        span = columns_of(shard, core, columns)
+        result = dot(rows_ref[...], weight[:, span]) + total_ref[:, span]
+        out_ref[:, shard] = result.reshape(groups, capacity, columns)
 
 
 def output_own(rows, weight, total, shape):
@@ -381,7 +409,6 @@
     packed, place = pack_rows(row_tenant, tenant_slot, activations, groups * capacity, per_store)
     arrived = swap(packed.reshape(groups, capacity, -1), "dp").reshape(packed.shape)
     base_query = jnp.dot(activations, query_weight, preferred_element_type=F32)
-    arrived, base_query = lax.optimization_barrier((arrived, base_query))
     other = across_chip(arrived)
     sent_query, facts = query_visit(
         arrived, other, query_deltas, query_where, base_query, groups

time: 82.7 us -> 81.9 us (level)
  blocking collectives: 49.5 us -> 66.2 us
  starting transfers between devices: 9.79 us -> 3.27 us
  waiting for transfers between devices: 6.5 us -> 0.6 us
  matrix products: 5.2 us -> 1.52 us
  Pallas kernels: 11.1 us -> 9.79 us
    all_to_all x3 -> x4, blocking collectives: 49.5 us -> 66.2 us  [swap(): return lax.all_to_all(blocks, axes, split_axis=0, concat_axis=0, tiled=True)]
    all_to_all x1 -> x0, starting transfers between devices: 6.87 us -> none  [swap(): return lax.all_to_all(blocks, axes, split_axis=0, concat_axis=0, tiled=True)]
    all_to_all x1 -> x0, waiting for transfers between devices: 4.36 us -> none  [swap(): return lax.all_to_all(blocks, axes, split_axis=0, concat_axis=0, tiled=True)]
    dot_general x1, matrix products: 5.2 us -> 1.52 us  [body(): base_query = jnp.dot(activations, query_weight, preferred_element_type=F32)]
    ppermute x2, waiting for transfers between devices: 2.14 us -> 0.6 us  [across_chip(): return lax.ppermute(block, 'tensor', [(i, i ^ 1) for i in range(count)])]
  transfers between devices with their start and end apart: 3 -> 2, of which waited for: 3 -> 1; matrix products, arithmetic and copies ran while one was open for 6% -> 2% of each run, Pallas kernels for 1% -> 1%
where the time goes in v4:
time: 81.9 us; the launch traced here: 81.8 us
  blocking collectives  66.2 us (81%)
  Pallas kernels  9.79 us (12%)
  starting transfers between devices  3.27 us (4%)
  matrix products  1.52 us (2%)
    all_to_all x4, blocking collectives, swap(): return lax.all_to_all(blocks, axes, split_axis=0, concat_axis=0, tiled=True)  66.2 us
    ppermute x2, starting transfers between devices, across_chip(): return lax.ppermute(block, 'tensor', [(i, i ^ 1) for i in range(count)])  3.27 us
    pallas_call x1, Pallas kernels, attend(): pl.pallas_call(attend_kernel, out_shape=jax.ShapeDtypeStruct((groups, sha...  2.4 us
    pallas_call x1, Pallas kernels, output_visit(): pl.pallas_call(output_kernel, out_shape=(jax.ShapeDtypeStruct((groups, sh...  2.12 us
    pallas_call x1, Pallas kernels, pack_rows(): pl.pallas_call(functools.partial(pack_kernel, per_store), out_shape=(jax....  1.83 us
    pallas_call x1, Pallas kernels, query_visit(): pl.pallas_call(functools.partial(query_kernel, base.shape[0]), out_shape=...  1.71 us
  transfers between devices with their start and end apart: 2, of which 1 were waited for; matrix products, arithmetic and copies ran while one was open for 2% of the time, Pallas kernels for 1%

profile of v4, /device:TPU:1, one launch (start us, length us, event | category | flops | bytes accessed | tf_op | source)
XLA Modules:
  0.0 81.8 jit_solution(16287841970111141551)
XLA Ops:
  0.0 0.0 copy-start.8
  0.0 0.0 copy-start.9
  0.0 1.8 %pack_rows.1 = (bf16[64,4352]{1,0:T(8,128)(2,1)S(1)}, bf16[64,32]{1,0:T(8,128)(2,1)S(1)}) custom-call(s32[1,32]{1,0:T(1,128)} %bitcast.23, s32[1,64]{1,0:T(1,128)} %bitcast.24, bf16[32,8192]{1,0:T(8,128)(2,1)} %rows_hbm.1), custom_call_target="tpu_custom_call" | custom-call | flops 34359738368 | bytes 50331648 | tf_op jit(solution)/shard_map/pack_rows/pallas_call | solution.py:101
  1.8 16.3 %all_to_all.34 = bf16[8,8,4352]{2,1,0:T(8,128)(2,1)S(1)} all-to-all(bf16[8,8,4352]{2,1,0:T(8,128)(2,1)S(1)} %bitcast.15), channel_id=1, replica_groups=mesh['dp'=8,'tensor'=16] {'dp'}, dimensions={0} | all-to-all | bytes 1114112 | tf_op jit(solution)/shard_map/all_to_all | solution.py:387
  18.1 0.0 copy-start.2
  18.2 0.0 copy-start.5
  18.2 2.2 %collective-permute-start = (bf16[64,4352]{1,0:T(8,128)(2,1)S(1)}, bf16[64,4352]{1,0:T(8,128)(2,1)S(1)}, u32[]{:S(2)}, u32[]{:S(2)}) collective-permute-start(bf16[64,4352]{1,0:T(8,128)(2,1)S(1)} %bitcast.13), channel_id=1, source_target_pairs={{0,1},{1,0},{2,3},{3,2},{4,5},{5,4},{6,7},{7,6},{8,9},{9,8},{10,11... | collective-permute-start | bytes 1671176 | tf_op jit(solution)/shard_map/ppermute | solution.py:383
  20.4 0.0 copy-done.8
  20.4 0.0 copy-done.9
  20.4 1.5 %fusion = f32[32,512]{1,0:T(8,128)S(1)} fusion(bf16[32,8192]{1,0:T(8,128)(2,1)S(1)} %copy-done.9, bf16[8192,512]{1,0:T(8,128)(2,1)S(1)} %copy-done.8), kind=kOutput, calls=%fused_computation.1 | convolution fusion | flops 268435456 | bytes 8978432 | tf_op jit(solution)/shard_map/dot_general | solution.py:411
  21.9 0.0 copy-start
  21.9 0.0 copy-start.1
  21.9 0.0 copy-start.4
  21.9 0.0 copy-start.7
  22.0 0.0 collective-permute-done.other_ref
  22.0 0.0 copy-done.2
  22.0 0.0 copy-done.5
  22.0 0.0 slice-start
  22.0 1.7 %query_visit.1 = (bf16[1024,128]{1,0:T(8,128)(2,1)S(1)}, f32[64,128]{1,0:T(8,128)S(1)}) custom-call(s32[8,8]{1,0:T(8,128)S(1)} %copy-done.5, bf16[64,4352]{1,0:T(8,128)(2,1)S(1)} %bitcast.14, bf16[64,4352]{1,0:T(8,128)(2,1)S(1)} %collective-permute-done.other_ref, bf16[8,8,128,128]{3,2,1,0:T(8,128)(2,1)S(1)} %copy-done.2, f32[128,128]{1,0:T(8,128)S(1)} %reshape.37.base_ref), custom_call_target="tpu_custom_call" | custom-call | flops 34359738368 | bytes 50331648 | tf_op jit(solution)/shard_map/query_visit/pallas_call | solution.py:185
  23.7 18.0 %all_to_all.35 = bf16[128,8,128]{2,1,0:T(8,128)(2,1)S(1)} all-to-all(bf16[128,8,128]{2,1,0:T(8,128)(2,1)S(1)} %bitcast.17), channel_id=1, replica_groups=mesh['dp'=8,'tensor'=16] {'dp','tensor'}, dimensions={0} | all-to-all | bytes 524288 | tf_op jit(solution)/shard_map/all_to_all | solution.py:387
  41.7 0.0 slice-start.1
  41.7 0.0 copy-done
  41.7 0.0 copy-done.1
  41.7 0.0 copy-done.4
  41.7 0.0 copy-done.7
  41.7 0.0 copy-start.3
  41.7 0.0 copy-start.6
  41.7 2.4 %attend.1 = bf16[8,16,8,128]{3,2,1,0:T(8,128)(2,1)S(1)} custom-call(s32[2]{0:T(128)S(1)} %copy-done.7, bf16[8,16,8,128]{3,2,1,0:T(8,128)(2,1)S(1)} %bitcast.18, bf16[2,2,1024]{2,1,0:T(2,128)(2,1)S(1)} %copy-done.4, bf16[2,8,1024,128]{3,2,1,0:T(8,128)(2,1)S(1)} %copy-done, bf16[2,8,1024,128]{3,2,1,0:T(8,128)(2,1)S(1)} %copy-done.1), custom_call_target="tpu_custom_call" | custom-call | flops 34359738368 | bytes 50331648 | tf_op jit(solution)/shard_map/attend/pallas_call | solution.py:259
  44.2 15.0 %all_to_all.36 = bf16[128,8,128]{2,1,0:T(8,128)(2,1)S(1)} all-to-all(bf16[128,8,128]{2,1,0:T(8,128)(2,1)S(1)} %bitcast.19), channel_id=1, replica_groups=mesh['dp'=8,'tensor'=16] {'dp','tensor'}, dimensions={0} | all-to-all | bytes 524288 | tf_op jit(solution)/shard_map/all_to_all | solution.py:387
  59.1 0.0 slice-done
  59.1 0.0 slice-done.1
  59.1 0.0 copy-done.3
  59.1 0.0 copy-done.6
  59.1 2.1 %output_visit.1 = (bf16[8,16,8,256]{3,2,1,0:T(8,128)(2,1)S(1)}, bf16[64,512]{1,0:T(8,128)(2,1)S(1)}, f32[64,8192]{1,0:T(8,128)S(1)}) custom-call(s32[8,8]{1,0:T(8,128)S(1)} %copy-done.6, bf16[1024,128]{1,0:T(8,128)(2,1)S(1)} %bitcast.16, f32[64,128]{1,0:T(8,128)S(1)} %get-tuple-element.14.facts_ref, bf16[8,8,128,128]{3,2,1,0:T(8,128)(2,1)S(1)} %copy-done.3, ...), custom_call_target="tpu_custom_call" | custom-call | flops 34359738368 | bytes 50331648 | tf_op jit(solution)/shard_map/output_visit/pallas_call | solution.py:322
  61.3 1.1 %collective-permute-start.1 = (bf16[8,16,8,256]{3,2,1,0:T(8,128)(2,1)S(1)}, bf16[8,16,8,256]{3,2,1,0:T(8,128)(2,1)S(1)}, u32[]{:S(2)}, u32[]{:S(2)}) collective-permute-start(bf16[8,16,8,256]{3,2,1,0:T(8,128)(2,1)S(1)} %get-tuple-element.17), channel_id=1, source_target_pairs={{0,1},{1,0},{2,3},{3,2},{4,5},{5,4},{6,7},{7,6},{8,9},{9,8},{10,11... | collective-permute-start | bytes 1572872 | tf_op jit(solution)/shard_map/ppermute | solution.py:383
  62.3 0.9 %output_own.1 = f32[8,16,8,256]{3,2,1,0:T(8,128)S(1)} custom-call(bf16[64,512]{1,0:T(8,128)(2,1)S(1)} %get-tuple-element.15.rows_ref, bf16[512,8192]{1,0:T(8,128)(2,1)S(1)} %bitcast.21, f32[64,8192]{1,0:T(8,128)S(1)} %get-tuple-element.16.total_ref), custom_call_target="tpu_custom_call" | custom-call | flops 34359738368 | bytes 50331648 | tf_op jit(solution)/shard_map/output_own/pallas_call | solution.py:349
  63.3 0.6 collective-permute-done.1
  63.9 0.1 add_convert_fusion
  64.0 17.0 %all_to_all.37 = bf16[128,8,256]{2,1,0:T(8,128)(2,1)S(1)} all-to-all(bf16[128,8,256]{2,1,0:T(8,128)(2,1)S(1)} %bitcast.22), channel_id=1, replica_groups=mesh['dp'=8,'tensor'=16] {'dp','tensor'}, dimensions={0} | all-to-all | bytes 1048576 | tf_op jit(solution)/shard_map/all_to_all | solution.py:387
  81.0 0.8 finish.1
  (2 shorter events, 0.0 us)
Async XLA Ops:
  0.0 20.4 %copy-start.8 = (bf16[8192,512]{1,0:T(8,128)(2,1)S(1)}, bf16[8192,512]{1,0:T(8,128)(2,1)}, u32[]{:S(2)}) copy-start(bf16[8192,512]{1,0:T(8,128)(2,1)} %param.14) | copy-start | bytes 25165828
  0.0 20.4 %copy-start.9 = (bf16[32,8192]{1,0:T(8,128)(2,1)S(1)}, bf16[32,8192]{1,0:T(8,128)(2,1)}, u32[]{:S(2)}) copy-start(bf16[32,8192]{1,0:T(8,128)(2,1)} %rows_hbm.1) | copy-start | bytes 1572868
  18.1 3.8 %copy-start.2 = (bf16[8,8,128,128]{3,2,1,0:T(8,128)(2,1)S(1)}, bf16[8,8,128,128]{3,2,1,0:T(8,128)(2,1)}, u32[]{:S(2)}) copy-start(bf16[8,8,128,128]{3,2,1,0:T(8,128)(2,1)} %tiles_ref.2) | copy-start | bytes 6291460
  18.2 3.8 %copy-start.5 = (s32[8,8]{1,0:T(8,128)S(1)}, s32[8,8]{1,0:T(8,128)}, u32[]{:S(2)}) copy-start(s32[8,8]{1,0:T(8,128)} %where_vmem.2) | copy-start | bytes 772
  18.2 3.8 %collective-permute-start = (bf16[64,4352]{1,0:T(8,128)(2,1)S(1)}, bf16[64,4352]{1,0:T(8,128)(2,1)S(1)}, u32[]{:S(2)}, u32[]{:S(2)}) collective-permute-start(bf16[64,4352]{1,0:T(8,128)(2,1)S(1)} %bitcast.13), channel_id=1, source_target_pairs={{0,1},{1,0},{2,3},{3,2},{4,5},{5,4},{6,7},{7,6},{8,9},{9,8},{10,11... | collective-permute-start | bytes 1671176 | tf_op jit(solution)/shard_map/ppermute | solution.py:383
  21.9 19.8 %copy-start = (bf16[2,8,1024,128]{3,2,1,0:T(8,128)(2,1)S(1)}, bf16[2,8,1024,128]{3,2,1,0:T(8,128)(2,1)}, u32[]{:S(2)}) copy-start(bf16[2,8,1024,128]{3,2,1,0:T(8,128)(2,1)} %keys.1) | copy-start | bytes 12582916
  21.9 19.8 %copy-start.1 = (bf16[2,8,1024,128]{3,2,1,0:T(8,128)(2,1)S(1)}, bf16[2,8,1024,128]{3,2,1,0:T(8,128)(2,1)}, u32[]{:S(2)}) copy-start(bf16[2,8,1024,128]{3,2,1,0:T(8,128)(2,1)} %values.1) | copy-start | bytes 12582916
  21.9 19.8 %copy-start.4 = (bf16[2,2,1024]{2,1,0:T(2,128)(2,1)S(1)}, bf16[2,2,1024]{2,1,0:T(2,128)(2,1)}, u32[]{:S(2)}) copy-start(bf16[2,2,1024]{2,1,0:T(2,128)(2,1)} %fresh_ref.1) | copy-start | bytes 24580
  21.9 19.8 %copy-start.7 = (s32[2]{0:T(128)S(1)}, s32[2]{0:T(128)}, u32[]{:S(2)}) copy-start(s32[2]{0:T(128)} %length_vmem.1) | copy-start | bytes 28
  22.0 37.1 %slice-start = ((s8[8388608]{0:T(1024)(128)(4,1)}), s8[4194304]{0:T(1024)(128)(4,1)S(1)}, s32[]{:S(2)}) async-start(s8[8388608]{0:T(1024)(128)(4,1)} %bitcast.20), calls=%async_computation.4 | async-start | bytes 8388608
  41.7 17.4 %slice-start.1 = ((s8[8388608]{0:T(1024)(128)(4,1)}), s8[4194304]{0:T(1024)(128)(4,1)S(1)}, s32[]{:S(2)}) async-start(s8[8388608]{0:T(1024)(128)(4,1)} %bitcast.20), calls=%async_computation.5 | async-start | bytes 8388608
  41.7 17.4 %copy-start.3 = (bf16[8,8,128,128]{3,2,1,0:T(8,128)(2,1)S(1)}, bf16[8,8,128,128]{3,2,1,0:T(8,128)(2,1)}, u32[]{:S(2)}) copy-start(bf16[8,8,128,128]{3,2,1,0:T(8,128)(2,1)} %tiles_ref.3) | copy-start | bytes 6291460
  41.7 17.4 %copy-start.6 = (s32[8,8]{1,0:T(8,128)S(1)}, s32[8,8]{1,0:T(8,128)}, u32[]{:S(2)}) copy-start(s32[8,8]{1,0:T(8,128)} %where_vmem.3) | copy-start | bytes 772
  61.3 2.6 %collective-permute-start.1 = (bf16[8,16,8,256]{3,2,1,0:T(8,128)(2,1)S(1)}, bf16[8,16,8,256]{3,2,1,0:T(8,128)(2,1)S(1)}, u32[]{:S(2)}, u32[]{:S(2)}) collective-permute-start(bf16[8,16,8,256]{3,2,1,0:T(8,128)(2,1)S(1)} %get-tuple-element.17), channel_id=1, source_target_pairs={{0,1},{1,0},{2,3},{3,2},{4,5},{5,4},{6,7},{7,6},{8,9},{9,8},{10,11... | collective-permute-start | bytes 1572872 | tf_op jit(solution)/shard_map/ppermute | solution.py:383

commit v5 on v4

--- a/solution.py
+++ b/solution.py
@@ -120,37 +120,54 @@
     )
 
 
-def query_kernel(
-    group_rows, where_vmem, mine_ref, other_ref, tiles_ref, base_ref, out_ref, facts_ref, where_ref, sem, expand, *totals
-):
-    fetch = pltpu.make_async_copy(where_vmem, where_ref, sem)
-    fetch.start()
-    me = lax.axis_index("dp")
-    core = lax.axis_index("tensor") % CORES
-    slots, per_slot, tile = tiles_ref.shape[:3]
+def route_kernel(group_rows, blocks, mine_ref, expand, facts_ref):
+    groups = lax.axis_size("dp")
     places = mine_ref.shape[0]
     width = mine_ref.shape[1] - 2 * LANES
-    halves = width // tile
-    groups = lax.axis_size("dp")
-    blocks = base_ref.shape[0] // group_rows
     capacity = places // groups
-    facts = mine_ref[:, width + LANES : width + 2 * LANES].astype(F32)
-    facts_ref[...] = facts
-    own_slot = facts[:, 0:1].astype(I32) - 1 - me * slots
+    block_rows = group_rows * blocks
     by_lane = mine_ref[:, width : width + LANES].astype(F32)
     by_lane = jnp.sum(by_lane.reshape(groups, capacity, LANES), axis=0)[0:1].astype(I32)
     lane = iota((1, LANES), 1)
     home = (lane % places) // capacity * group_rows + by_lane - 1
     home = jnp.where(by_lane > 0, home * blocks + lane // places, -blocks)
-    block_rows = group_rows * blocks
     for g in range(groups):
         row = iota((block_rows, LANES), 0) + g * block_rows
         for n, b in enumerate(range(0, blocks, LANES // places)):
             one_hot = pick(row == home + b).astype(BF16)
             expand[g * block_rows : (g + 1) * block_rows, n * LANES : (n + 1) * LANES] = one_hot
+    facts_ref[...] = mine_ref[:, width + LANES : width + 2 * LANES].astype(F32)
+
+
+def routes(mine, groups, group_rows, blocks):
+    places = mine.shape[0]
+    homes = groups * group_rows * blocks
+    vmem = pl.BlockSpec(memory_space=pltpu.VMEM)
+    return pl.pallas_call(
+        functools.partial(route_kernel, group_rows, blocks),
+        out_shape=(
+            jax.ShapeDtypeStruct((homes, places * blocks), BF16),
+            jax.ShapeDtypeStruct((places, LANES), F32),
+        ),
+        in_specs=[vmem],
+        out_specs=(vmem, vmem),
+        compiler_params=pltpu.CompilerParams(vmem_limit_bytes=8 << 20),
+        name="routes",
+    )(mine)
+
+
+def query_kernel(
+    where_ref, mine_ref, other_ref, facts_ref, tiles_ref, out_ref, *totals
+):
+    me = lax.axis_index("dp")
+    core = lax.axis_index("tensor") % CORES
+    slots, per_slot, tile = tiles_ref.shape[:3]
+    width = mine_ref.shape[1] - 2 * LANES
+    halves = width // tile
+    blocks = totals[0].shape[1] // tile
+    own_slot = facts_ref[:, 0:1].astype(I32) - 1 - me * slots
     for total in totals:
         total[...] = jnp.zeros_like(total)
-    fetch.wait()
     for t in range(slots):
         mine = own_slot == t
         for k in range(per_slot):
@@ -168,44 +185,50 @@
     for total in totals[1:]:
         whole = whole + total[...]
     sums = [whole[:, b * tile : (b + 1) * tile] for b in range(blocks)]
-    stacked = jnp.concatenate(sums, axis=0).astype(BF16)
-    for g in range(groups):
-        span = slice(g * block_rows, (g + 1) * block_rows)
-        sent = dot(expand[span, :], stacked) + jnp.where(me == g, base_ref[...], 0.0)
-        out_ref[span, :] = sent.astype(BF16)
-
-
-def query_visit(mine, other, tiles, where, base, groups):
+    out_ref[...] = jnp.concatenate(sums, axis=0).astype(BF16)
+
+
+def query_visit(mine, other, facts, tiles, where, columns):
     places = mine.shape[0]
     tile = tiles.shape[2]
-    columns = base.shape[1]
-    blocks = columns // tile
-    stacked = base.reshape(base.shape[0] * blocks, tile)
-    vmem = pl.BlockSpec(memory_space=pltpu.VMEM)
-    return pl.pallas_call(
-        functools.partial(query_kernel, base.shape[0]),
-        out_shape=(
-            jax.ShapeDtypeStruct((groups * stacked.shape[0], tile), BF16),
-            jax.ShapeDtypeStruct((places, LANES), F32),
-        ),
+    vmem = pl.BlockSpec(memory_space=pltpu.VMEM)
+    return pl.pallas_call(
+        query_kernel,
+        out_shape=jax.ShapeDtypeStruct((places * columns // tile, tile), BF16),
         in_specs=[vmem] * 5,
-        scratch_shapes=[
-            pltpu.SMEM(where.shape, I32),
-            pltpu.SemaphoreType.DMA,
-            pltpu.VMEM((groups * stacked.shape[0], places * blocks), BF16),
-        ]
-        + [pltpu.VMEM((places, columns), F32)] * 4,
+        out_specs=vmem,
+        scratch_shapes=[pltpu.VMEM((places, columns), F32)] * 4,
+        compiler_params=pltpu.CompilerParams(vmem_limit_bytes=4 << 20),
+        name="query_visit",
+    )(where, mine, other, facts, tiles)
+
+
+def send_kernel(expand, stacked_ref, base_ref, out_ref):
+    me = lax.axis_index("dp")
+    block_rows = base_ref.shape[0]
+    for g in range(out_ref.shape[0] // block_rows):
+        span = slice(g * block_rows, (g + 1) * block_rows)
+        sent = dot(expand[span, :], stacked_ref[...]) + jnp.where(me == g, base_ref[...], 0.0)
+        out_ref[span, :] = sent.astype(BF16)
+
+
+def query_send(expand, stacked, base):
+    tile = stacked.shape[1]
+    vmem = pl.BlockSpec(memory_space=pltpu.VMEM)
+    return pl.pallas_call(
+        send_kernel,
+        out_shape=jax.ShapeDtypeStruct((expand.shape[0], tile), BF16),
+        in_specs=[vmem] * 3,
+        out_specs=vmem,
         cost_estimate=COST,
-        compiler_params=pltpu.CompilerParams(vmem_limit_bytes=12 << 20),
-        name="query_visit",
-    )(where, mine, other, tiles, stacked)
+        compiler_params=pltpu.CompilerParams(vmem_limit_bytes=4 << 20),
+        name="query_send",
+    )(expand, stacked, base.reshape(-1, tile))
 
 
 def attend_kernel(
-    length_vmem, arrived_ref, fresh_ref, keys, values, out_ref, length_ref, sem
+    length_ref, arrived_ref, fresh_ref, keys, values, out_ref, raw
 ):
-    fetch = pltpu.make_async_copy(length_vmem, length_ref, sem)
-    fetch.start()
     requests, kv_heads, context, size = keys.shape
     shards = out_ref.shape[1]
     stores = arrived_ref.shape[0]
@@ -216,19 +239,21 @@
     fresh = fresh_ref[...].astype(F32)
     upper = iota((8, size), 0) < 4
     position = iota((1, context), 1)
-    fetch.wait()
     mixed = [[None] * kv_heads for _ in range(requests)]
     for i in range(requests):
-        visible = position < length_ref[i]
-        parts = []
+        heads_of = []
         for g in range(kv_heads):
             first, second = query[2 * g], query[2 * g + 1]
             if i == 0:
                 heads = jnp.where(upper, first, pltpu.roll(second, 4, 0))
             else:
                 heads = jnp.where(upper, pltpu.roll(first, 4, 0), second)
-            heads = heads.astype(BF16)
-            scores = dot(heads, keys[i, g], ((1,), (1,))) * scale
+            heads_of.append(heads.astype(BF16))
+            raw[g] = dot(heads_of[g], keys[i, g], ((1,), (1,))) * scale
+        visible = position < length_ref[0, i]
+        parts = []
+        for g in range(kv_heads):
+            heads, scores = heads_of[g], raw[g]
             fresh_key = fresh[i, 0:1, g * size : (g + 1) * size]
             own = jnp.sum(heads.astype(F32) * fresh_key, axis=1, keepdims=True) * scale
             scores = jnp.where(visible, scores, -1e30)
@@ -260,18 +285,17 @@
         attend_kernel,
         out_shape=jax.ShapeDtypeStruct((groups, shards, 8, size), BF16),
         in_specs=[vmem] * 5,
-        scratch_shapes=[pltpu.SMEM(lengths.shape, I32), pltpu.SemaphoreType.DMA],
-        cost_estimate=COST,
-        compiler_params=pltpu.CompilerParams(vmem_limit_bytes=16 << 20),
+        scratch_shapes=[
+            pltpu.VMEM((kv_heads, 8, context), F32),
+        ],
+        compiler_params=pltpu.CompilerParams(vmem_limit_bytes=4 << 20),
         name="attend",
-    )(lengths, arrived.reshape(groups, shards, 8, size), fresh, keys, values)
+    )(lengths.reshape(1, -1), arrived.reshape(groups, shards, 8, size), fresh, keys, values)
 
 
 def output_kernel(
-    where_vmem, arrived_ref, facts_ref, tiles_ref, weight, out_ref, rows_ref, total_ref, where_ref, sem, hold
+    where_ref, arrived_ref, facts_ref, tiles_ref, weight, out_ref, rows_ref, total_ref, hold
 ):
-    fetch = pltpu.make_async_copy(where_vmem, where_ref, sem)
-    fetch.start()
     me = lax.axis_index("dp")
     other = 1 - lax.axis_index("tensor") % CORES
     slots, per_slot, tile = tiles_ref.shape[:3]
@@ -292,7 +316,6 @@
     for b in range(blocks):
         rows_ref[:, b * tile : (b + 1) * tile] = gathered[b * places : (b + 1) * places]
     targets = width // tile
-    fetch.wait()
     every = slots * per_slot // shards
     for shard in range(shards):
         for n in range(shard * every, (shard + 1) * every):
@@ -328,7 +351,7 @@
         ),
         in_specs=[vmem] * 5,
         out_specs=(vmem, vmem, vmem),
-        scratch_shapes=[pltpu.SMEM(where.shape, I32), pltpu.SemaphoreType.DMA, pltpu.VMEM((shards, places, depth // CORES), F32)],
+        scratch_shapes=[pltpu.VMEM((shards, places, depth // CORES), F32)],
         cost_estimate=COST,
         compiler_params=pltpu.CompilerParams(vmem_limit_bytes=16 << 20),
         name="output_visit",
@@ -410,9 +433,12 @@
     arrived = swap(packed.reshape(groups, capacity, -1), "dp").reshape(packed.shape)
     base_query = jnp.dot(activations, query_weight, preferred_element_type=F32)
     other = across_chip(arrived)
-    sent_query, facts = query_visit(
-        arrived, other, query_deltas, query_where, base_query, groups
-    )
+    blocks = base_query.shape[1] // LANES
+    expand, facts = routes(arrived, groups, activations.shape[0], blocks)
+    products = query_visit(
+        arrived, other, facts, query_deltas, query_where, base_query.shape[1]
+    )
+    sent_query = query_send(expand, products, base_query)
     query = swap(sent_query, EVERY)
     attended = attend(query, key_cache, value_cache, fresh_pair, cache_length, groups)
     size = attended.shape[3]

time: 81.9 us -> 80.8 us (0.987)
  Pallas kernels: 9.79 us -> 8.64 us
    pallas_call x1 -> x3, Pallas kernels: 1.71 us -> 1.31 us  [the longest x1 0.89 us: query_visit(): pl.pallas_call(query_kernel, out_shape=jax.ShapeDtypeStruct((places * col...]
where the time goes in v5:
time: 80.8 us; the launch traced here: 80.6 us
  blocking collectives  66.1 us (82%)
  Pallas kernels  8.64 us (11%)
  starting transfers between devices  3.34 us (4%)
  matrix products  1.52 us (2%)
    all_to_all x4, blocking collectives, swap(): return lax.all_to_all(blocks, axes, split_axis=0, concat_axis=0, tiled=True)  66.1 us
    ppermute x2, starting transfers between devices, across_chip(): return lax.ppermute(block, 'tensor', [(i, i ^ 1) for i in range(count)])  3.34 us
    pallas_call x1, Pallas kernels, output_visit(): pl.pallas_call(output_kernel, out_shape=(jax.ShapeDtypeStruct((groups, sh...  1.92 us
    pallas_call x1, Pallas kernels, attend(): pl.pallas_call(attend_kernel, out_shape=jax.ShapeDtypeStruct((groups, sha...  1.85 us
    pallas_call x1, Pallas kernels, pack_rows(): pl.pallas_call(functools.partial(pack_kernel, per_store), out_shape=(jax....  1.83 us
  transfers between devices with their start and end apart: 2, of which 1 were waited for; matrix products, arithmetic and copies ran while one was open for 2% of the time, Pallas kernels for 1%

profile of v5, /device:TPU:1, one launch (start us, length us, event | category | flops | bytes accessed | tf_op | source)
XLA Modules:
  0.0 80.6 jit_solution(4369695022683643174)
XLA Ops:
  0.0 0.0 copy-start.8
  0.0 0.0 copy-start.9
  0.0 1.8 %pack_rows.1 = (bf16[64,4352]{1,0:T(8,128)(2,1)S(1)}, bf16[64,32]{1,0:T(8,128)(2,1)S(1)}) custom-call(s32[1,32]{1,0:T(1,128)} %bitcast.26, s32[1,64]{1,0:T(1,128)} %bitcast.27, bf16[32,8192]{1,0:T(8,128)(2,1)} %rows_hbm.1), custom_call_target="tpu_custom_call" | custom-call | flops 34359738368 | bytes 50331648 | tf_op jit(solution)/shard_map/pack_rows/pallas_call | solution.py:101
  1.8 16.3 %all_to_all.34 = bf16[8,8,4352]{2,1,0:T(8,128)(2,1)S(1)} all-to-all(bf16[8,8,4352]{2,1,0:T(8,128)(2,1)S(1)} %bitcast.19), channel_id=1, replica_groups=mesh['dp'=8,'tensor'=16] {'dp'}, dimensions={0} | all-to-all | bytes 1114112 | tf_op jit(solution)/shard_map/all_to_all | solution.py:410
  18.1 0.0 copy-start.2
  18.2 0.0 copy-start.4
  18.2 2.2 %collective-permute-start = (bf16[64,4352]{1,0:T(8,128)(2,1)S(1)}, bf16[64,4352]{1,0:T(8,128)(2,1)S(1)}, u32[]{:S(2)}, u32[]{:S(2)}) collective-permute-start(bf16[64,4352]{1,0:T(8,128)(2,1)S(1)} %bitcast.13), channel_id=1, source_target_pairs={{0,1},{1,0},{2,3},{3,2},{4,5},{5,4},{6,7},{7,6},{8,9},{9,8},{10,11... | collective-permute-start | bytes 1671176 | tf_op jit(solution)/shard_map/ppermute | solution.py:406
  20.4 0.0 copy-done.8
  20.4 0.0 copy-done.9
  20.4 1.5 %fusion = f32[32,512]{1,0:T(8,128)S(1)} fusion(bf16[32,8192]{1,0:T(8,128)(2,1)S(1)} %copy-done.9, bf16[8192,512]{1,0:T(8,128)(2,1)S(1)} %copy-done.8), kind=kOutput, calls=%fused_computation.1 | convolution fusion | flops 268435456 | bytes 8978432 | tf_op jit(solution)/shard_map/dot_general | solution.py:434
  21.9 0.1 routes.1
  22.1 0.0 collective-permute-done.other_ref
  22.1 0.0 copy-done.2
  22.1 0.0 copy-done.4
  22.1 0.9 %query_visit.1.stacked_ref = bf16[256,128]{1,0:T(8,128)(2,1)S(1)} custom-call(s32[8,8]{1,0:T(8,128)S(1)} %copy-done.4, bf16[64,4352]{1,0:T(8,128)(2,1)S(1)} %bitcast.15, bf16[64,4352]{1,0:T(8,128)(2,1)S(1)} %collective-permute-done.other_ref, f32[64,128]{1,0:T(8,128)S(1)} %get-tuple-element.14.facts_ref, bf16[8,8,128,128]{3,2,1,0:T(8,128)(2,1)S(1)} %copy-done.2), custom_call_target="tpu_custom_call" | custom-call | tf_op jit(solution)/shard_map/query_visit/pallas_call | solution.py:195
  23.0 0.0 slice-start
  23.0 0.0 copy-start
  23.0 0.0 copy-start.1
  23.0 0.0 copy-start.3
  23.0 0.0 copy-start.5
  23.0 0.0 slice-start.1
  23.1 0.3 query_send.1
  23.3 0.0 copy-start.6
  23.4 0.0 copy-start.7
  23.4 17.9 %all_to_all.35 = bf16[128,8,128]{2,1,0:T(8,128)(2,1)S(1)} all-to-all(bf16[128,8,128]{2,1,0:T(8,128)(2,1)S(1)} %bitcast.21), channel_id=1, replica_groups=mesh['dp'=8,'tensor'=16] {'dp','tensor'}, dimensions={0} | all-to-all | bytes 524288 | tf_op jit(solution)/shard_map/all_to_all | solution.py:410
  41.3 0.0 copy-done
  41.3 0.0 copy-done.1
  41.3 0.0 copy-done.3
  41.3 0.0 copy-done.5
  41.3 1.8 %attend.1 = bf16[8,16,8,128]{3,2,1,0:T(8,128)(2,1)S(1)} custom-call(s32[1,2]{1,0:T(1,128)S(1)} %bitcast.22, bf16[8,16,8,128]{3,2,1,0:T(8,128)(2,1)S(1)} %bitcast.17, bf16[2,2,1024]{2,1,0:T(2,128)(2,1)S(1)} %copy-done.3, bf16[2,8,1024,128]{3,2,1,0:T(8,128)(2,1)S(1)} %copy-done, bf16[2,8,1024,128]{3,2,1,0:T(8,128)(2,1)S(1)} %copy-done.1), custom_call_target="tpu_custom_call" | custom-call | tf_op jit(solution)/shard_map/attend/pallas_call | solution.py:284
  43.1 15.0 %all_to_all.36 = bf16[128,8,128]{2,1,0:T(8,128)(2,1)S(1)} all-to-all(bf16[128,8,128]{2,1,0:T(8,128)(2,1)S(1)} %bitcast.18), channel_id=1, replica_groups=mesh['dp'=8,'tensor'=16] {'dp','tensor'}, dimensions={0} | all-to-all | bytes 524288 | tf_op jit(solution)/shard_map/all_to_all | solution.py:410
  58.1 0.0 slice-done
  58.1 0.0 slice-done.1
  58.1 0.0 copy-done.6
  58.1 0.0 copy-done.7
  58.1 1.9 %output_visit.1 = (bf16[8,16,8,256]{3,2,1,0:T(8,128)(2,1)S(1)}, bf16[64,512]{1,0:T(8,128)(2,1)S(1)}, f32[64,8192]{1,0:T(8,128)S(1)}) custom-call(s32[8,8]{1,0:T(8,128)S(1)} %copy-done.7, bf16[1024,128]{1,0:T(8,128)(2,1)S(1)} %bitcast.20, f32[64,128]{1,0:T(8,128)S(1)} %get-tuple-element.14.facts_ref, bf16[8,8,128,128]{3,2,1,0:T(8,128)(2,1)S(1)} %copy-done.6, ...), custom_call_target="tpu_custom_call" | custom-call | flops 34359738368 | bytes 50331648 | tf_op jit(solution)/shard_map/output_visit/pallas_call | solution.py:345
  60.1 1.1 %collective-permute-start.1 = (bf16[8,16,8,256]{3,2,1,0:T(8,128)(2,1)S(1)}, bf16[8,16,8,256]{3,2,1,0:T(8,128)(2,1)S(1)}, u32[]{:S(2)}, u32[]{:S(2)}) collective-permute-start(bf16[8,16,8,256]{3,2,1,0:T(8,128)(2,1)S(1)} %get-tuple-element.17), channel_id=1, source_target_pairs={{0,1},{1,0},{2,3},{3,2},{4,5},{5,4},{6,7},{7,6},{8,9},{9,8},{10,11... | collective-permute-start | bytes 1572872 | tf_op jit(solution)/shard_map/ppermute | solution.py:406
  61.2 0.9 %output_own.1 = f32[8,16,8,256]{3,2,1,0:T(8,128)S(1)} custom-call(bf16[64,512]{1,0:T(8,128)(2,1)S(1)} %get-tuple-element.15.rows_ref, bf16[512,8192]{1,0:T(8,128)(2,1)S(1)} %bitcast.24, f32[64,8192]{1,0:T(8,128)S(1)} %get-tuple-element.16.total_ref), custom_call_target="tpu_custom_call" | custom-call | flops 34359738368 | bytes 50331648 | tf_op jit(solution)/shard_map/output_own/pallas_call | solution.py:372
  62.1 0.6 collective-permute-done.1
  62.7 0.1 add_convert_fusion
  62.9 16.9 %all_to_all.37 = bf16[128,8,256]{2,1,0:T(8,128)(2,1)S(1)} all-to-all(bf16[128,8,256]{2,1,0:T(8,128)(2,1)S(1)} %bitcast.25), channel_id=1, replica_groups=mesh['dp'=8,'tensor'=16] {'dp','tensor'}, dimensions={0} | all-to-all | bytes 1048576 | tf_op jit(solution)/shard_map/all_to_all | solution.py:410
  79.8 0.8 %finish.1 = bf16[32,512]{1,0:T(8,128)(2,1)} custom-call(bf16[8,8,2,8,256]{4,3,2,1,0:T(8,128)(2,1)S(1)} %bitcast.16, bf16[64,32]{1,0:T(8,128)(2,1)S(1)} %get-tuple-element.18.place_ref), custom_call_target="tpu_custom_call" | custom-call | tf_op jit(solution)/shard_map/finish/pallas_call | solution.py:396
  (2 shorter events, 0.0 us)
Async XLA Ops:
  0.0 20.4 %copy-start.8 = (bf16[8192,512]{1,0:T(8,128)(2,1)S(1)}, bf16[8192,512]{1,0:T(8,128)(2,1)}, u32[]{:S(2)}) copy-start(bf16[8192,512]{1,0:T(8,128)(2,1)} %param.14) | copy-start | bytes 25165828
  0.0 20.4 %copy-start.9 = (bf16[32,8192]{1,0:T(8,128)(2,1)S(1)}, bf16[32,8192]{1,0:T(8,128)(2,1)}, u32[]{:S(2)}) copy-start(bf16[32,8192]{1,0:T(8,128)(2,1)} %rows_hbm.1) | copy-start | bytes 1572868
  18.1 3.9 %copy-start.2 = (bf16[8,8,128,128]{3,2,1,0:T(8,128)(2,1)S(1)}, bf16[8,8,128,128]{3,2,1,0:T(8,128)(2,1)}, u32[]{:S(2)}) copy-start(bf16[8,8,128,128]{3,2,1,0:T(8,128)(2,1)} %tiles_ref.2) | copy-start | bytes 6291460
  18.2 3.9 %copy-start.4 = (s32[8,8]{1,0:T(8,128)S(1)}, s32[8,8]{1,0:T(8,128)}, u32[]{:S(2)}) copy-start(s32[8,8]{1,0:T(8,128)} %where_ref.2) | copy-start | bytes 772
  18.2 3.9 %collective-permute-start = (bf16[64,4352]{1,0:T(8,128)(2,1)S(1)}, bf16[64,4352]{1,0:T(8,128)(2,1)S(1)}, u32[]{:S(2)}, u32[]{:S(2)}) collective-permute-start(bf16[64,4352]{1,0:T(8,128)(2,1)S(1)} %bitcast.13), channel_id=1, source_target_pairs={{0,1},{1,0},{2,3},{3,2},{4,5},{5,4},{6,7},{7,6},{8,9},{9,8},{10,11... | collective-permute-start | bytes 1671176 | tf_op jit(solution)/shard_map/ppermute | solution.py:406
  23.0 35.1 %slice-start = ((s8[8388608]{0:T(1024)(128)(4,1)}), s8[4194304]{0:T(1024)(128)(4,1)S(1)}, s32[]{:S(2)}) async-start(s8[8388608]{0:T(1024)(128)(4,1)} %bitcast.23), calls=%async_computation.4 | async-start | bytes 8388608
  23.0 18.3 %copy-start = (bf16[2,8,1024,128]{3,2,1,0:T(8,128)(2,1)S(1)}, bf16[2,8,1024,128]{3,2,1,0:T(8,128)(2,1)}, u32[]{:S(2)}) copy-start(bf16[2,8,1024,128]{3,2,1,0:T(8,128)(2,1)} %keys.1) | copy-start | bytes 12582916
  23.0 18.3 %copy-start.1 = (bf16[2,8,1024,128]{3,2,1,0:T(8,128)(2,1)S(1)}, bf16[2,8,1024,128]{3,2,1,0:T(8,128)(2,1)}, u32[]{:S(2)}) copy-start(bf16[2,8,1024,128]{3,2,1,0:T(8,128)(2,1)} %values.1) | copy-start | bytes 12582916
  23.0 18.3 %copy-start.3 = (bf16[2,2,1024]{2,1,0:T(2,128)(2,1)S(1)}, bf16[2,2,1024]{2,1,0:T(2,128)(2,1)}, u32[]{:S(2)}) copy-start(bf16[2,2,1024]{2,1,0:T(2,128)(2,1)} %fresh_ref.1) | copy-start | bytes 24580
  23.0 18.3 %copy-start.5 = (s32[2]{0:T(128)S(1)}, s32[2]{0:T(128)}, u32[]{:S(2)}) copy-start(s32[2]{0:T(128)} %param.19) | copy-start | bytes 28
  23.0 35.1 %slice-start.1 = ((s8[8388608]{0:T(1024)(128)(4,1)}), s8[4194304]{0:T(1024)(128)(4,1)S(1)}, s32[]{:S(2)}) async-start(s8[8388608]{0:T(1024)(128)(4,1)} %bitcast.23), calls=%async_computation.5 | async-start | bytes 8388608
  23.3 34.8 %copy-start.6 = (bf16[8,8,128,128]{3,2,1,0:T(8,128)(2,1)S(1)}, bf16[8,8,128,128]{3,2,1,0:T(8,128)(2,1)}, u32[]{:S(2)}) copy-start(bf16[8,8,128,128]{3,2,1,0:T(8,128)(2,1)} %tiles_ref.3) | copy-start | bytes 6291460
  23.4 34.8 %copy-start.7 = (s32[8,8]{1,0:T(8,128)S(1)}, s32[8,8]{1,0:T(8,128)}, u32[]{:S(2)}) copy-start(s32[8,8]{1,0:T(8,128)} %where_ref.3) | copy-start | bytes 772
  60.1 2.7 %collective-permute-start.1 = (bf16[8,16,8,256]{3,2,1,0:T(8,128)(2,1)S(1)}, bf16[8,16,8,256]{3,2,1,0:T(8,128)(2,1)S(1)}, u32[]{:S(2)}, u32[]{:S(2)}) collective-permute-start(bf16[8,16,8,256]{3,2,1,0:T(8,128)(2,1)S(1)} %get-tuple-element.17), channel_id=1, source_target_pairs={{0,1},{1,0},{2,3},{3,2},{4,5},{5,4},{6,7},{7,6},{8,9},{9,8},{10,11... | collective-permute-start | bytes 1572872 | tf_op jit(solution)/shard_map/ppermute | solution.py:406

commit v6 on v5

--- a/solution.py
+++ b/solution.py
@@ -240,34 +240,39 @@
     upper = iota((8, size), 0) < 4
     position = iota((1, context), 1)
     mixed = [[None] * kv_heads for _ in range(requests)]
-    for i in range(requests):
-        heads_of = []
-        for g in range(kv_heads):
-            first, second = query[2 * g], query[2 * g + 1]
-            if i == 0:
-                heads = jnp.where(upper, first, pltpu.roll(second, 4, 0))
-            else:
-                heads = jnp.where(upper, pltpu.roll(first, 4, 0), second)
-            heads_of.append(heads.astype(BF16))
-            raw[g] = dot(heads_of[g], keys[i, g], ((1,), (1,))) * scale
+    heads_of = {}
+
+    def score(i, g):
+        first, second = query[2 * g], query[2 * g + 1]
+        if i == 0:
+            heads = jnp.where(upper, first, pltpu.roll(second, 4, 0))
+        else:
+            heads = jnp.where(upper, pltpu.roll(first, 4, 0), second)
+        heads_of[i, g] = heads.astype(BF16)
+        raw[i, g] = dot(heads_of[i, g], keys[i, g], ((1,), (1,))) * scale
+
+    def soften(i, g):
         visible = position < length_ref[0, i]
-        parts = []
-        for g in range(kv_heads):
-            heads, scores = heads_of[g], raw[g]
-            fresh_key = fresh[i, 0:1, g * size : (g + 1) * size]
-            own = jnp.sum(heads.astype(F32) * fresh_key, axis=1, keepdims=True) * scale
-            scores = jnp.where(visible, scores, -1e30)
-            highest = jnp.maximum(jnp.max(scores, axis=1, keepdims=True), own)
-            weights = jnp.where(visible, jnp.exp(scores - highest), 0.0)
-            own_weight = jnp.exp(own - highest)
-            total = jnp.sum(weights, axis=1, keepdims=True) + own_weight
-            share = (weights / total).astype(BF16)
-            own_share = (own_weight / total).astype(BF16).astype(F32)
-            parts.append((share, own_share))
-        for g in range(kv_heads):
-            share, own_share = parts[g]
-            fresh_value = fresh[i, 1:2, g * size : (g + 1) * size]
-            mixed[i][g] = dot(share, values[i, g]) + own_share * fresh_value
+        heads, scores = heads_of[i, g], raw[i, g]
+        fresh_key = fresh[i, 0:1, g * size : (g + 1) * size]
+        own = jnp.sum(heads.astype(F32) * fresh_key, axis=1, keepdims=True) * scale
+        scores = jnp.where(visible, scores, -1e30)
+        highest = jnp.maximum(jnp.max(scores, axis=1, keepdims=True), own)
+        weights = jnp.where(visible, jnp.exp(scores - highest), 0.0)
+        own_weight = jnp.exp(own - highest)
+        inverse = 1.0 / (jnp.sum(weights, axis=1, keepdims=True) + own_weight)
+        share = (weights * inverse).astype(BF16)
+        own_share = (own_weight * inverse).astype(BF16).astype(F32)
+        fresh_value = fresh[i, 1:2, g * size : (g + 1) * size]
+        mixed[i][g] = dot(share, values[i, g]) + own_share * fresh_value
+
+    units = [(i, g) for i in range(requests) for g in range(kv_heads)]
+    ahead = 3
+    for n in range(len(units) + ahead):
+        if n < len(units):
+            score(*units[n])
+        if n >= ahead:
+            soften(*units[n - ahead])
     for g in range(kv_heads):
         one, two = mixed[0][g], mixed[1][g]
         first = jnp.where(upper, one, pltpu.roll(two, 4, 0)).astype(BF16)
@@ -286,7 +291,7 @@
         out_shape=jax.ShapeDtypeStruct((groups, shards, 8, size), BF16),
         in_specs=[vmem] * 5,
         scratch_shapes=[
-            pltpu.VMEM((kv_heads, 8, context), F32),
+            pltpu.VMEM((requests, kv_heads, 8, context), F32),
         ],
         compiler_params=pltpu.CompilerParams(vmem_limit_bytes=4 << 20),
         name="attend",
@@ -303,18 +308,19 @@
     places = groups * capacity
     depth, width = weight.shape
     blocks = depth // tile
-    group_rows = arrived_ref.shape[0] // (groups * blocks)
-    facts = facts_ref[...].astype(I32)
-    own_slot = facts[:, 0:1] - 1 - me * slots
-    number = facts[:, 1:2]
-    home = iota((places, 1), 0) // capacity * group_rows + number - 1
-    home = jnp.where(number > 0, home * blocks, -blocks)
+    own_slot = facts_ref[:, 0:1].astype(I32) - 1 - me * slots
     total_ref[...] = jnp.zeros_like(total_ref)
-    lane = iota((places, arrived_ref.shape[0]), 1)
-    gather = jnp.concatenate([pick(lane == home + b).astype(BF16) for b in range(blocks)], axis=0)
-    gathered = dot(gather, arrived_ref[...]).astype(BF16)
+    span = arrived_ref.shape[0] // groups
+    lane = iota((capacity, span), 1)
+    taken = []
+    for g in range(groups):
+        number = facts_ref[g * capacity : (g + 1) * capacity, 1:2].astype(I32)
+        home = jnp.where(number > 0, (number - 1) * blocks, -blocks)
+        take = jnp.concatenate([pick(lane == home + b) for b in range(blocks)], axis=0)
+        taken.append(dot(take.astype(BF16), arrived_ref[g * span : (g + 1) * span, :]))
     for b in range(blocks):
-        rows_ref[:, b * tile : (b + 1) * tile] = gathered[b * places : (b + 1) * places]
+        block = [piece[b * capacity : (b + 1) * capacity] for piece in taken]
+        rows_ref[:, b * tile : (b + 1) * tile] = jnp.concatenate(block, axis=0).astype(BF16)
     targets = width // tile
     every = slots * per_slot // shards
     for shard in range(shards):

time: 80.8 us -> 81 us (level)
  no operation moved by 1% of the time
where the time goes in v6:
time: 81 us; the launch traced here: 80.8 us
  blocking collectives  66.1 us (82%)
  Pallas kernels  8.86 us (11%)
  starting transfers between devices  3.34 us (4%)
  matrix products  1.52 us (2%)
    all_to_all x4, blocking collectives, swap(): return lax.all_to_all(blocks, axes, split_axis=0, concat_axis=0, tiled=True)  66.1 us
    ppermute x2, starting transfers between devices, across_chip(): return lax.ppermute(block, 'tensor', [(i, i ^ 1) for i in range(count)])  3.34 us
    pallas_call x1, Pallas kernels, attend(): pl.pallas_call(attend_kernel, out_shape=jax.ShapeDtypeStruct((groups, sha...  2.11 us
    pallas_call x1, Pallas kernels, output_visit(): pl.pallas_call(output_kernel, out_shape=(jax.ShapeDtypeStruct((groups, sh...  1.86 us
    pallas_call x1, Pallas kernels, pack_rows(): pl.pallas_call(functools.partial(pack_kernel, per_store), out_shape=(jax....  1.83 us
  transfers between devices with their start and end apart: 2, of which 1 were waited for; matrix products, arithmetic and copies ran while one was open for 2% of the time, Pallas kernels for 1%

profile of v6, /device:TPU:1, one launch (start us, length us, event | category | flops | bytes accessed | tf_op | source)
XLA Modules:
  0.0 80.8 jit_solution(9888546615728617529)
XLA Ops:
  0.0 0.0 copy-start.8
  0.0 0.0 copy-start.9
  0.0 1.8 %pack_rows.1 = (bf16[64,4352]{1,0:T(8,128)(2,1)S(1)}, bf16[64,32]{1,0:T(8,128)(2,1)S(1)}) custom-call(s32[1,32]{1,0:T(1,128)} %bitcast.26, s32[1,64]{1,0:T(1,128)} %bitcast.27, bf16[32,8192]{1,0:T(8,128)(2,1)} %rows_hbm.1), custom_call_target="tpu_custom_call" | custom-call | flops 34359738368 | bytes 50331648 | tf_op jit(solution)/shard_map/pack_rows/pallas_call | solution.py:101
  1.8 16.3 %all_to_all.34 = bf16[8,8,4352]{2,1,0:T(8,128)(2,1)S(1)} all-to-all(bf16[8,8,4352]{2,1,0:T(8,128)(2,1)S(1)} %bitcast.19), channel_id=1, replica_groups=mesh['dp'=8,'tensor'=16] {'dp'}, dimensions={0} | all-to-all | bytes 1114112 | tf_op jit(solution)/shard_map/all_to_all | solution.py:416
  18.1 0.0 copy-start.2
  18.2 0.0 copy-start.4
  18.2 2.2 %collective-permute-start = (bf16[64,4352]{1,0:T(8,128)(2,1)S(1)}, bf16[64,4352]{1,0:T(8,128)(2,1)S(1)}, u32[]{:S(2)}, u32[]{:S(2)}) collective-permute-start(bf16[64,4352]{1,0:T(8,128)(2,1)S(1)} %bitcast.13), channel_id=1, source_target_pairs={{0,1},{1,0},{2,3},{3,2},{4,5},{5,4},{6,7},{7,6},{8,9},{9,8},{10,11... | collective-permute-start | bytes 1671176 | tf_op jit(solution)/shard_map/ppermute | solution.py:412
  20.4 0.0 copy-done.8
  20.4 0.0 copy-done.9
  20.4 1.5 %fusion = f32[32,512]{1,0:T(8,128)S(1)} fusion(bf16[32,8192]{1,0:T(8,128)(2,1)S(1)} %copy-done.9, bf16[8192,512]{1,0:T(8,128)(2,1)S(1)} %copy-done.8), kind=kOutput, calls=%fused_computation.1 | convolution fusion | flops 268435456 | bytes 8978432 | tf_op jit(solution)/shard_map/dot_general | solution.py:440
  21.9 0.1 routes.1
  22.1 0.0 collective-permute-done.other_ref
  22.1 0.0 copy-done.2
  22.1 0.0 copy-done.4
  22.1 0.9 %query_visit.1.stacked_ref = bf16[256,128]{1,0:T(8,128)(2,1)S(1)} custom-call(s32[8,8]{1,0:T(8,128)S(1)} %copy-done.4, bf16[64,4352]{1,0:T(8,128)(2,1)S(1)} %bitcast.15, bf16[64,4352]{1,0:T(8,128)(2,1)S(1)} %collective-permute-done.other_ref, f32[64,128]{1,0:T(8,128)S(1)} %get-tuple-element.14.facts_ref, bf16[8,8,128,128]{3,2,1,0:T(8,128)(2,1)S(1)} %copy-done.2), custom_call_target="tpu_custom_call" | custom-call | tf_op jit(solution)/shard_map/query_visit/pallas_call | solution.py:195
  23.0 0.0 slice-start
  23.0 0.0 copy-start
  23.0 0.0 copy-start.1
  23.0 0.0 copy-start.3
  23.0 0.0 copy-start.5
  23.1 0.0 slice-start.1
  23.1 0.3 query_send.1
  23.4 0.0 copy-start.6
  23.4 0.0 copy-start.7
  23.4 17.9 %all_to_all.35 = bf16[128,8,128]{2,1,0:T(8,128)(2,1)S(1)} all-to-all(bf16[128,8,128]{2,1,0:T(8,128)(2,1)S(1)} %bitcast.21), channel_id=1, replica_groups=mesh['dp'=8,'tensor'=16] {'dp','tensor'}, dimensions={0} | all-to-all | bytes 524288 | tf_op jit(solution)/shard_map/all_to_all | solution.py:416
  41.3 0.0 copy-done
  41.3 0.0 copy-done.1
  41.3 0.0 copy-done.3
  41.3 0.0 copy-done.5
  41.3 2.1 %attend.1 = bf16[8,16,8,128]{3,2,1,0:T(8,128)(2,1)S(1)} custom-call(s32[1,2]{1,0:T(1,128)S(1)} %bitcast.22, bf16[8,16,8,128]{3,2,1,0:T(8,128)(2,1)S(1)} %bitcast.17, bf16[2,2,1024]{2,1,0:T(2,128)(2,1)S(1)} %copy-done.3, bf16[2,8,1024,128]{3,2,1,0:T(8,128)(2,1)S(1)} %copy-done, bf16[2,8,1024,128]{3,2,1,0:T(8,128)(2,1)S(1)} %copy-done.1), custom_call_target="tpu_custom_call" | custom-call | tf_op jit(solution)/shard_map/attend/pallas_call | solution.py:289
  43.4 15.0 %all_to_all.36 = bf16[128,8,128]{2,1,0:T(8,128)(2,1)S(1)} all-to-all(bf16[128,8,128]{2,1,0:T(8,128)(2,1)S(1)} %bitcast.18), channel_id=1, replica_groups=mesh['dp'=8,'tensor'=16] {'dp','tensor'}, dimensions={0} | all-to-all | bytes 524288 | tf_op jit(solution)/shard_map/all_to_all | solution.py:416
  58.4 0.0 slice-done
  58.4 0.0 slice-done.1
  58.4 0.0 copy-done.6
  58.4 0.0 copy-done.7
  58.4 1.9 %output_visit.1 = (bf16[8,16,8,256]{3,2,1,0:T(8,128)(2,1)S(1)}, bf16[64,512]{1,0:T(8,128)(2,1)S(1)}, f32[64,8192]{1,0:T(8,128)S(1)}) custom-call(s32[8,8]{1,0:T(8,128)S(1)} %copy-done.7, bf16[1024,128]{1,0:T(8,128)(2,1)S(1)} %bitcast.20, f32[64,128]{1,0:T(8,128)S(1)} %get-tuple-element.14.facts_ref, bf16[8,8,128,128]{3,2,1,0:T(8,128)(2,1)S(1)} %copy-done.6, ...), custom_call_target="tpu_custom_call" | custom-call | flops 34359738368 | bytes 50331648 | tf_op jit(solution)/shard_map/output_visit/pallas_call | solution.py:351
  60.3 1.1 %collective-permute-start.1 = (bf16[8,16,8,256]{3,2,1,0:T(8,128)(2,1)S(1)}, bf16[8,16,8,256]{3,2,1,0:T(8,128)(2,1)S(1)}, u32[]{:S(2)}, u32[]{:S(2)}) collective-permute-start(bf16[8,16,8,256]{3,2,1,0:T(8,128)(2,1)S(1)} %get-tuple-element.17), channel_id=1, source_target_pairs={{0,1},{1,0},{2,3},{3,2},{4,5},{5,4},{6,7},{7,6},{8,9},{9,8},{10,11... | collective-permute-start | bytes 1572872 | tf_op jit(solution)/shard_map/ppermute | solution.py:412
  61.4 0.9 %output_own.1 = f32[8,16,8,256]{3,2,1,0:T(8,128)S(1)} custom-call(bf16[64,512]{1,0:T(8,128)(2,1)S(1)} %get-tuple-element.15.rows_ref, bf16[512,8192]{1,0:T(8,128)(2,1)S(1)} %bitcast.24, f32[64,8192]{1,0:T(8,128)S(1)} %get-tuple-element.16.total_ref), custom_call_target="tpu_custom_call" | custom-call | flops 34359738368 | bytes 50331648 | tf_op jit(solution)/shard_map/output_own/pallas_call | solution.py:378
  62.3 0.6 collective-permute-done.1
  62.9 0.1 add_convert_fusion
  63.1 17.0 %all_to_all.37 = bf16[128,8,256]{2,1,0:T(8,128)(2,1)S(1)} all-to-all(bf16[128,8,256]{2,1,0:T(8,128)(2,1)S(1)} %bitcast.25), channel_id=1, replica_groups=mesh['dp'=8,'tensor'=16] {'dp','tensor'}, dimensions={0} | all-to-all | bytes 1048576 | tf_op jit(solution)/shard_map/all_to_all | solution.py:416
  80.0 0.8 finish.1
  (2 shorter events, 0.0 us)
Async XLA Ops:
  0.0 20.4 %copy-start.8 = (bf16[8192,512]{1,0:T(8,128)(2,1)S(1)}, bf16[8192,512]{1,0:T(8,128)(2,1)}, u32[]{:S(2)}) copy-start(bf16[8192,512]{1,0:T(8,128)(2,1)} %param.14) | copy-start | bytes 25165828
  0.0 20.4 %copy-start.9 = (bf16[32,8192]{1,0:T(8,128)(2,1)S(1)}, bf16[32,8192]{1,0:T(8,128)(2,1)}, u32[]{:S(2)}) copy-start(bf16[32,8192]{1,0:T(8,128)(2,1)} %rows_hbm.1) | copy-start | bytes 1572868
  18.1 3.9 %copy-start.2 = (bf16[8,8,128,128]{3,2,1,0:T(8,128)(2,1)S(1)}, bf16[8,8,128,128]{3,2,1,0:T(8,128)(2,1)}, u32[]{:S(2)}) copy-start(bf16[8,8,128,128]{3,2,1,0:T(8,128)(2,1)} %tiles_ref.2) | copy-start | bytes 6291460
  18.2 3.9 %copy-start.4 = (s32[8,8]{1,0:T(8,128)S(1)}, s32[8,8]{1,0:T(8,128)}, u32[]{:S(2)}) copy-start(s32[8,8]{1,0:T(8,128)} %where_ref.2) | copy-start | bytes 772
  18.2 3.9 %collective-permute-start = (bf16[64,4352]{1,0:T(8,128)(2,1)S(1)}, bf16[64,4352]{1,0:T(8,128)(2,1)S(1)}, u32[]{:S(2)}, u32[]{:S(2)}) collective-permute-start(bf16[64,4352]{1,0:T(8,128)(2,1)S(1)} %bitcast.13), channel_id=1, source_target_pairs={{0,1},{1,0},{2,3},{3,2},{4,5},{5,4},{6,7},{7,6},{8,9},{9,8},{10,11... | collective-permute-start | bytes 1671176 | tf_op jit(solution)/shard_map/ppermute | solution.py:412
  23.0 35.4 %slice-start = ((s8[8388608]{0:T(1024)(128)(4,1)}), s8[4194304]{0:T(1024)(128)(4,1)S(1)}, s32[]{:S(2)}) async-start(s8[8388608]{0:T(1024)(128)(4,1)} %bitcast.23), calls=%async_computation.4 | async-start | bytes 8388608
  23.0 18.3 %copy-start = (bf16[2,8,1024,128]{3,2,1,0:T(8,128)(2,1)S(1)}, bf16[2,8,1024,128]{3,2,1,0:T(8,128)(2,1)}, u32[]{:S(2)}) copy-start(bf16[2,8,1024,128]{3,2,1,0:T(8,128)(2,1)} %keys.1) | copy-start | bytes 12582916
  23.0 18.3 %copy-start.1 = (bf16[2,8,1024,128]{3,2,1,0:T(8,128)(2,1)S(1)}, bf16[2,8,1024,128]{3,2,1,0:T(8,128)(2,1)}, u32[]{:S(2)}) copy-start(bf16[2,8,1024,128]{3,2,1,0:T(8,128)(2,1)} %values.1) | copy-start | bytes 12582916
  23.0 18.2 %copy-start.3 = (bf16[2,2,1024]{2,1,0:T(2,128)(2,1)S(1)}, bf16[2,2,1024]{2,1,0:T(2,128)(2,1)}, u32[]{:S(2)}) copy-start(bf16[2,2,1024]{2,1,0:T(2,128)(2,1)} %fresh_ref.1) | copy-start | bytes 24580
  23.0 18.2 %copy-start.5 = (s32[2]{0:T(128)S(1)}, s32[2]{0:T(128)}, u32[]{:S(2)}) copy-start(s32[2]{0:T(128)} %param.19) | copy-start | bytes 28
  23.1 35.3 %slice-start.1 = ((s8[8388608]{0:T(1024)(128)(4,1)}), s8[4194304]{0:T(1024)(128)(4,1)S(1)}, s32[]{:S(2)}) async-start(s8[8388608]{0:T(1024)(128)(4,1)} %bitcast.23), calls=%async_computation.5 | async-start | bytes 8388608
  23.4 35.0 %copy-start.6 = (bf16[8,8,128,128]{3,2,1,0:T(8,128)(2,1)S(1)}, bf16[8,8,128,128]{3,2,1,0:T(8,128)(2,1)}, u32[]{:S(2)}) copy-start(bf16[8,8,128,128]{3,2,1,0:T(8,128)(2,1)} %tiles_ref.3) | copy-start | bytes 6291460
  23.4 35.0 %copy-start.7 = (s32[8,8]{1,0:T(8,128)S(1)}, s32[8,8]{1,0:T(8,128)}, u32[]{:S(2)}) copy-start(s32[8,8]{1,0:T(8,128)} %where_ref.3) | copy-start | bytes 772
  60.3 2.7 %collective-permute-start.1 = (bf16[8,16,8,256]{3,2,1,0:T(8,128)(2,1)S(1)}, bf16[8,16,8,256]{3,2,1,0:T(8,128)(2,1)S(1)}, u32[]{:S(2)}, u32[]{:S(2)}) collective-permute-start(bf16[8,16,8,256]{3,2,1,0:T(8,128)(2,1)S(1)} %get-tuple-element.17), channel_id=1, source_target_pairs={{0,1},{1,0},{2,3},{3,2},{4,5},{5,4},{6,7},{7,6},{8,9},{9,8},{10,11... | collective-permute-start | bytes 1572872 | tf_op jit(solution)/shard_map/ppermute | solution.py:412
